TPU v7x, 32 devices: a whole 2x2x4 slice. The times are simulated.
32 devices in a mesh: ctx: 8 (over z, x), exp: 4 (over y, core).
Axes of the slice: x: 2, y: 2, z: 4, core: 2. Of those that a mesh axis runs over, the one named last changes fastest.
Arguments:
- attn_query: bfloat16 [8192, 2048], P('ctx', 'exp'), may hold values from -112 to 112
- attn_key: bfloat16 [8192, 2048], P('ctx', 'exp'), may hold values from -40 to 40
- attn_value: bfloat16 [8192, 2048], P('ctx', 'exp'), may hold values from -40 to 40
- prefix_state: float32 [8, 16, 128, 128], P('ctx', 'exp'), may hold values from -40960 to 40960
- moe_in: bfloat16 [8192, 2048], P(('ctx', 'exp')), may hold values from -6 to 6
- grad_out: bfloat16 [8192, 2048], P(('ctx', 'exp')), may hold values from -6 to 6
- router_gates: bfloat16 [8192, 1], P(('ctx', 'exp')), may hold values from 0.099609375 to 1
- expert_ids: int32 [8192, 1], P(('ctx', 'exp')), may hold values from 0 to 3; in each aligned block of 256 rows (0 to 255, 256 to 511, ...) at most 96 rows name the same one
- w_gate_up: bfloat16 [4, 2048, 1024], P('exp'), may hold values from -0.125 to 0.125
- w_down: bfloat16 [4, 512, 2048], P('exp'), may hold values from -0.25 to 0.25
- w_out: bfloat16 [2048, 2048], P('exp'), may hold values from -0.125 to 0.125
Outputs:
- grad_query: bfloat16 [8192, 2048], P('ctx', 'exp')
- grad_key: bfloat16 [8192, 2048], P('ctx', 'exp')
- grad_value: bfloat16 [8192, 2048], P('ctx', 'exp')
- grad_resid: bfloat16 [8192, 2048], P(('ctx', 'exp'))
- grad_gates: bfloat16 [8192, 1], P(('ctx', 'exp'))
- grad_gate_up: float32 [4, 2048, 1024], P('exp', 'ctx')
- grad_down: float32 [4, 512, 2048], P('exp', 'ctx')
Inputs may be any that keep to these rules, and one draw needn't show every extreme that they name: `expert_ids`: among the 256 rows of one device (aligned blocks of rows) no expert is named more than 96 times, a bound that some block reaches.
All inputs are finite; a program needn't handle non-finite values.
Results may differ from a plain program's by a relative error of at most 0.0063.
Values may be sent and summed in bfloat16 or wider, within the bound.
A program may use at most 192 MiB of HBM per device.

v0:
```python
import functools

import jax
import jax.numpy as jnp
from jax import lax
from jax.experimental import pallas as pl
from jax.experimental.pallas import tpu as pltpu
from jax.sharding import PartitionSpec as P

LANES = 128


def contract_rows(left, right):
    return lax.dot_general(
        left, right, (((0,), (0,)), ((), ())), preferred_element_type=jnp.float32
    )


def contract_cols(left, right):
    return lax.dot_general(
        left, right, (((1,), (1,)), ((), ())), preferred_element_type=jnp.float32
    )


def plain(left, right):
    return jnp.dot(left, right, preferred_element_type=jnp.float32)


def flip(value, axis, bit, size):
    return lax.ppermute(value, axis, [(i, i ^ bit) for i in range(size)])


def expert_kernel(near, width, *refs):
    blocks, (pair_ref, back_ref) = refs[:near], refs[near : near + 2]
    rows_ref, hidden_ref, scaled_ref, both_ref = refs[near + 2 : near + 6]
    outs = refs[near + 6 :]
    capacity = blocks[0].shape[0]
    hidden_units = back_ref.shape[0]
    for at, block in enumerate(blocks):
        rows_ref[pl.ds(at * capacity, capacity), :] = block[:, :width]
    cot_wide = jnp.concatenate([block[:, width : 2 * width] for block in blocks], axis=0).astype(
        jnp.float32
    )
    gate_vals = jnp.concatenate([block[:, 2 * width :] for block in blocks], axis=0)
    scaled = (gate_vals[:, :1].astype(jnp.float32) * cot_wide).astype(jnp.bfloat16)
    scaled_ref[...] = scaled
    both = plain(rows_ref[...], pair_ref[...])
    first = both[:, :hidden_units]
    second = both[:, hidden_units:]
    logistic = jax.nn.sigmoid(first)
    silu = first * logistic
    hidden = (silu * second).astype(jnp.bfloat16)
    hidden_ref[...] = hidden
    grad_hidden = contract_cols(scaled, back_ref[...])
    slope = logistic * (1.0 + first * (1.0 - logistic))
    both_ref[:, :hidden_units] = (grad_hidden * second * slope).astype(jnp.bfloat16)
    both_ref[:, hidden_units:] = (grad_hidden * silu).astype(jnp.bfloat16)
    output = plain(hidden, back_ref[...])
    grad_gate = jnp.sum(cot_wide * output, axis=1, keepdims=True)
    grad_rows = contract_cols(both_ref[...], pair_ref[...]).astype(jnp.bfloat16)
    for at, out in enumerate(outs):
        rows = slice(at * capacity, (at + 1) * capacity)
        out[:, :width] = grad_rows[rows]
        out[:, width:] = jnp.broadcast_to(grad_gate[rows], (capacity, LANES)).astype(jnp.bfloat16)


def expert_backward(blocks, width, w_pair, w_back):
    near = len(blocks)
    capacity = blocks[0].shape[0]
    tokens = near * capacity
    hidden_units = w_back.shape[0]

    def shape(*dims):
        return jax.ShapeDtypeStruct(dims, jnp.bfloat16)

    outs = [shape(tokens, width), shape(tokens, hidden_units), shape(tokens, width)]
    outs += [shape(tokens, 2 * hidden_units)] + [shape(capacity, width + LANES)] * near
    whole = pl.BlockSpec(memory_space=pltpu.VMEM)
    return pl.pallas_call(
        functools.partial(expert_kernel, near, width),
        in_specs=[whole] * (near + 2),
        out_specs=[whole] * len(outs),
        out_shape=outs,
        cost_estimate=cost(12 * tokens * width * hidden_units, 24 * hidden_units * width),
        name="expert",
    )(*blocks, w_pair, w_back)


def after(value, *others):
    return lax.optimization_barrier((value,) + others)[0]


def cost(flops, moved):
    return pl.CostEstimate(flops=flops, bytes_accessed=moved, transcendentals=0)


def partial_kernel(by_rows, parts, me_ref, *refs):
    lefts, rights, came, out_ref = refs[:parts], refs[parts : 2 * parts], refs[2 * parts : -1], refs[-1]
    multiply = plain if by_rows else contract_rows
    total = multiply(lefts[0][...], rights[0][...])
    for left_ref, right_ref in zip(lefts[1:], rights[1:]):
        total = total + multiply(left_ref[...], right_ref[...])
    for one in came:
        total = total + one[0].astype(jnp.float32)
    out_ref[0] = total.astype(out_ref.dtype)


class ScatterSum:
    def __init__(self, lefts, rights, at, cols, axis, bits, by_rows, rows):
        self.lefts, self.rights, self.at, self.cols = lefts, rights, at, cols
        self.axis, self.bits, self.by_rows = axis, bits, by_rows
        self.size = lax.axis_size(axis)
        self.unit = rows // self.size
        self.me = lax.axis_index(axis).astype(jnp.int32).reshape(1)
        self.came = []

    def step(self, *ties):
        bits, stage, unit, cols, at = self.bits, len(self.came), self.unit, self.cols, self.at
        last = stage == len(bits)
        free = sorted(set(bits) - set(bits[: stage + 1]))

        def chunk(j, me_ref):
            own = me_ref[0]
            found = 0
            for bit in bits[: stage + 1]:
                found = found | (own & (1 << bit))
            if not last:
                found = found ^ (1 << bits[stage])
            for place, bit in enumerate(free):
                found = found | (((j >> place) & 1) << bit)
            return found

        def spot(upto):
            kept = sorted(set(bits) - set(bits[:upto]))

            def index(j, me_ref):
                found = chunk(j, me_ref)
                where = 0 * j
                for place, bit in enumerate(kept):
                    where = where | (((found >> bit) & 1) << place)
                return (where, 0, 0)

            return index

        steps = 1 << len(free)
        depth = self.rights[0].shape[0]
        if self.by_rows:
            left_spec = pl.BlockSpec((unit, depth), lambda j, me_ref: (chunk(j, me_ref), 0))
        else:
            left_spec = pl.BlockSpec((depth, unit), lambda j, me_ref: (0, chunk(j, me_ref)))
        right_spec = pl.BlockSpec((depth, cols), lambda j, me_ref: (0, at))
        parts = len(self.lefts)
        came = self.came
        if ties and came:
            came = came[:-1] + [after(came[-1], *ties)]
        kind = jnp.float32 if last else jnp.bfloat16
        out = pl.pallas_call(
            functools.partial(partial_kernel, self.by_rows, parts),
            grid_spec=pltpu.PrefetchScalarGridSpec(
                num_scalar_prefetch=1,
                grid=(steps,),
                in_specs=[left_spec] * parts
                + [right_spec] * parts
                + [pl.BlockSpec((1, unit, cols), spot(i + 1)) for i in range(stage)],
                out_specs=pl.BlockSpec((1, unit, cols), lambda j, me_ref: (j, 0, 0)),
            ),
            out_shape=jax.ShapeDtypeStruct((steps, unit, cols), kind),
            cost_estimate=cost(2 * parts * depth * unit * cols * steps, 4 * steps * unit * cols + 2 * depth * cols),
        )(self.me, *self.lefts, *self.rights, *came)
        if last:
            return out
        self.came = came + [flip(out, self.axis, 1 << bits[stage], self.size)]
        return None


def state_kernel(query_ref, grad_ref, inv_ref, state_ref, scaled_ref):
    scaled = (grad_ref[...].astype(jnp.float32) * inv_ref[...]).astype(jnp.bfloat16)
    scaled_ref[...] = scaled
    state_ref[0] = contract_rows(query_ref[...], scaled)


def forward_kernel(chunk, key_ref, value_ref, grad_ref, inv_ref, prior_ref, out_ref):
    tokens = key_ref.shape[0]
    row = lax.broadcasted_iota(jnp.int32, (chunk, chunk), 0)
    col = lax.broadcasted_iota(jnp.int32, (chunk, chunk), 1)
    state = prior_ref[0]
    for at in range(tokens // chunk):
        rows = pl.ds(at * chunk, chunk)
        keys, values, grads = key_ref[rows, :], value_ref[rows, :], grad_ref[rows, :]
        mix = jnp.where(col <= row, contract_cols(grads, values), 0.0).astype(jnp.bfloat16)
        out = plain(mix, keys) + contract_cols(grads, state.astype(jnp.bfloat16))
        out_ref[rows, :] = (out * inv_ref[rows, :]).astype(jnp.bfloat16)
        state = state + contract_rows(keys, values)


def backward_kernel(chunk, query_ref, key_ref, value_ref, scaled_ref, later_ref, dkey_ref, dvalue_ref):
    tokens = key_ref.shape[0]
    row = lax.broadcasted_iota(jnp.int32, (chunk, chunk), 0)
    col = lax.broadcasted_iota(jnp.int32, (chunk, chunk), 1)
    state = later_ref[0]
    for at in reversed(range(tokens // chunk)):
        rows = pl.ds(at * chunk, chunk)
        query, keys, values, scaled = query_ref[rows, :], key_ref[rows, :], value_ref[rows, :], scaled_ref[rows, :]
        held = state.astype(jnp.bfloat16)
        mix_key = jnp.where(col >= row, contract_cols(values, scaled), 0.0).astype(jnp.bfloat16)
        dkey_ref[rows, :] = (plain(mix_key, query) + contract_cols(values, held)).astype(jnp.bfloat16)
        mix_value = jnp.where(col >= row, contract_cols(keys, query), 0.0).astype(jnp.bfloat16)
        dvalue_ref[rows, :] = (plain(mix_value, scaled) + plain(keys, held)).astype(jnp.bfloat16)
        state = state + contract_rows(query, scaled)


def compute(
    attn_query,
    attn_key,
    attn_value,
    prefix_state,
    moe_in,
    grad_out,
    router_gates,
    expert_ids,
    w_gate_up,
    w_down,
    w_out,
):
    groups = lax.axis_size("exp")
    blocks_total = lax.axis_size("ctx")
    flight = w_gate_up.shape[0] * groups
    rows, width = moe_in.shape
    capacity = 3 * rows // (2 * flight)
    flat_ids = expert_ids.reshape(rows)
    place = jnp.arange(rows, dtype=jnp.int32)
    same = (flat_ids[:, None] == flat_ids[None, :]) & (place[:, None] < place[None, :])
    slot_of = jnp.sum(same.astype(jnp.int32), axis=0)
    mine = lax.axis_index("exp")
    target = (flat_ids ^ mine) * capacity + slot_of
    joined = jnp.concatenate(
        [moe_in, grad_out, jnp.broadcast_to(router_gates, (rows, LANES))], axis=1
    )
    place = jnp.arange(capacity, dtype=jnp.int32)[:, None]
    placing = {
        k: (place + k * capacity == target[None, :]).astype(jnp.bfloat16) for k in range(groups)
    }
    arrived = {}
    for k in reversed(range(groups)):
        packed = plain(placing[k], joined).astype(jnp.bfloat16)
        arrived[k] = flip(packed, "exp", k, groups) if k else packed
    near = groups // 2
    parts, returned = [], {}
    for low in (0, near):
        chosen = range(low, low + near)
        found = expert_backward([arrived[k] for k in chosen], width, w_gate_up[0], w_down[0])
        for k in reversed(chosen):
            sent = found[4 + k - low]
            returned[k] = flip(sent, "exp", k, groups) if k else sent
        parts.append(found)

    levels = blocks_total.bit_length() - 1
    rising = list(range(levels))
    turned = rising[1:] + rising[:1]
    hidden_units = w_down.shape[1]
    by_rows = (width // blocks_total) % LANES != 0
    lefts = [part[0].T if by_rows else part[0] for part in parts]
    grad_boths = [part[3] for part in parts]
    ups = [
        ScatterSum(lefts, grad_boths, at, hidden_units, "ctx", rising, by_rows, width)
        for at in range(2)
    ]
    down = ScatterSum(
        [part[1].T for part in parts], [part[2] for part in parts],
        0, width, "ctx", turned, True, hidden_units,
    )
    for one in (ups[0], down, ups[1]):
        one.step()

    def unpack(low):
        chosen = range(low, low + near)
        return contract_rows(
            jnp.concatenate([placing[k] for k in chosen], axis=0),
            jnp.concatenate([returned[k] for k in chosen], axis=0),
        )

    pair_grads = unpack(0) + unpack(near)
    grad_resid = (grad_out.astype(jnp.float32) + pair_grads[:, :width]).astype(jnp.bfloat16)
    grad_gates = pair_grads[:, width : width + 1].astype(jnp.bfloat16)

    pieces = {0: grad_resid}
    heads_width = w_out.shape[0]
    attn_grad = jnp.zeros((rows * groups, heads_width), jnp.bfloat16)
    for k in range(1, groups):
        low = k & -k
        pieces[k] = flip(pieces[k - low], "exp", low, groups)
    for k in range(groups):
        piece = contract_cols(pieces[k], w_out).astype(jnp.bfloat16)
        attn_grad = lax.dynamic_update_slice(attn_grad, piece, ((mine ^ k) * rows, 0))
        if k == 0:
            ups[0].step(attn_grad)
            down.step(attn_grad)
    ups[1].step(attn_grad)

    head_dim = prefix_state.shape[-1]
    tokens = attn_query.shape[0]
    heads = attn_query.shape[1] // head_dim
    block_at = lax.axis_index("ctx")
    counts = (
        3 * tokens * blocks_total + block_at * tokens + jnp.arange(tokens, dtype=jnp.int32) + 1
    ).astype(jnp.float32)
    inverse = jnp.broadcast_to((1.0 / counts)[:, None], (tokens, head_dim))

    per_head = pl.BlockSpec((tokens, head_dim), lambda h: (0, h))
    fixed = pl.BlockSpec((tokens, head_dim), lambda h: (0, 0))
    one_state = pl.BlockSpec((1, head_dim, head_dim), lambda h: (h, 0, 0))
    flat = jax.ShapeDtypeStruct((tokens, heads * head_dim), jnp.bfloat16)
    states = jax.ShapeDtypeStruct((heads, head_dim, head_dim), jnp.float32)
    chunk = min(256, tokens)

    size = 2 * tokens * heads * head_dim
    local_state, grad_scaled = pl.pallas_call(
        state_kernel,
        grid=(heads,),
        in_specs=[per_head, per_head, fixed],
        out_specs=[one_state, per_head],
        out_shape=[states, flat],
        cost_estimate=cost(size * head_dim, 3 * size),
        name="state",
    )(attn_query, attn_grad, inverse)

    later = jnp.zeros_like(local_state)
    step = 1
    results = {}
    while step < blocks_total:
        held = (local_state + later).astype(jnp.bfloat16)
        came = lax.ppermute(held, "ctx", [(i, i - step) for i in range(step, blocks_total)])
        for name, one in (("up0", ups[0]), ("down", down), ("up1", ups[1])):
            if name not in results and (name != "up1" or step > 1):
                got = one.step(held)
                if got is not None:
                    results[name] = got
        later = later + came.astype(jnp.float32)
        step *= 2

    grad_query = pl.pallas_call(
        functools.partial(forward_kernel, chunk),
        grid=(heads,),
        in_specs=[per_head, per_head, per_head, fixed, one_state],
        out_specs=per_head,
        out_shape=flat,
        cost_estimate=cost(size * (2 * chunk + 2 * head_dim), 4 * size),
        name="forward",
    )(attn_key, attn_value, attn_grad, inverse, prefix_state[0])
    grad_key, grad_value = pl.pallas_call(
        functools.partial(backward_kernel, chunk),
        grid=(heads,),
        in_specs=[per_head, per_head, per_head, per_head, one_state],
        out_specs=[per_head, per_head],
        out_shape=[flat, flat],
        cost_estimate=cost(size * (4 * chunk + 3 * head_dim), 6 * size),
        name="backward",
    )(attn_query, attn_key, attn_value, grad_scaled, later)
    for name, one in (("up0", ups[0]), ("down", down), ("up1", ups[1])):
        while name not in results:
            got = one.step()
            if got is not None:
                results[name] = got
    grad_gate_up = jnp.concatenate([results["up0"], results["up1"]], axis=2)
    grad_down = results["down"]
    return grad_query, grad_key, grad_value, grad_resid, grad_gates, grad_gate_up, grad_down


def solution(mesh):
    return jax.shard_map(
        compute,
        mesh=mesh,
        in_specs=(
            P("ctx", "exp"),
            P("ctx", "exp"),
            P("ctx", "exp"),
            P("ctx", "exp", None, None),
            P(("ctx", "exp"), None),
            P(("ctx", "exp"), None),
            P(("ctx", "exp"), None),
            P(("ctx", "exp"), None),
            P("exp", None, None),
            P("exp", None, None),
            P("exp", None),
        ),
        out_specs=(
            P("ctx", "exp"),
            P("ctx", "exp"),
            P("ctx", "exp"),
            P(("ctx", "exp"), None),
            P(("ctx", "exp"), None),
            P("exp", "ctx", None),
            P("exp", "ctx", None),
        ),
        check_vma=False,
    )
```

profile of v0, /device:TPU:0, one launch (start us, length us, event | category | flops | bytes accessed | tf_op | source)
XLA Modules:
  0.0 202.3 jit_solution(10595344044686269312)
XLA Ops:
  0.7 1.0 convert_reduce_fusion
  2.3 0.7 reduce
  3.1 2.2 %convolution_convert_fusion.1 = bf16[96,4224]{1,0:T(8,128)(2,1)S(1)} fusion(s32[256]{0:T(256)S(1)} %multiply_add_fusion, s32[96]{0:T(128)S(1)} %get-tuple-element.76, bf16[256,128]{1,0:T(8,128)(2,1)S(1)} %broadcast_in_dim.10, bf16[256,2048]{1,0:T(8,128)(2,1)} %param.16, bf16[256,2048]{1,0:T(8,128)(2,1)} %param.15), kind=kOutput, calls=%fused_computation.1 | convolution fusion | flops 214536192 | bytes 2975104 | tf_op jit(solution)/shard_map/dot_general | solution.py:26
  5.4 3.1 %collective-permute-start.2 = (bf16[96,4224]{1,0:T(8,128)(2,1)S(1)}, bf16[96,4224]{1,0:T(8,128)(2,1)}, u32[]{:S(2)}, u32[]{:S(2)}) collective-permute-start(bf16[96,4224]{1,0:T(8,128)(2,1)S(1)} %convolution_convert_fusion.1), channel_id=1, source_target_pairs={{0,2},{1,3},{2,0},{3,1},{4,6},{5,7},{6,4},{7,5},{8,10},{9,11},{10,... | collective-permute-start | bytes 2433032 | tf_op jit(solution)/shard_map/ppermute | solution.py:30
  9.1 1.4 convolution_convert_fusion.2
  10.6 1.4 convolution_convert_fusion.3.refs_0_
  12.0 15.5 %collective-permute-done.2.refs_0_ = bf16[96,4224]{1,0:T(8,128)(2,1)} collective-permute-done((bf16[96,4224]{1,0:T(8,128)(2,1)S(1)}, bf16[96,4224]{1,0:T(8,128)(2,1)}, u32[]{:S(2)}, u32[]{:S(2)}) %collective-permute-start.2) | collective-permute-done | bytes 811040 | tf_op jit(solution)/shard_map/ppermute | solution.py:30
  27.4 15.7 %collective-permute-done.3.refs_1_ = bf16[96,4224]{1,0:T(8,128)(2,1)} collective-permute-done((bf16[96,4224]{1,0:T(8,128)(2,1)S(1)}, bf16[96,4224]{1,0:T(8,128)(2,1)}, u32[]{:S(2)}, u32[]{:S(2)}) %collective-permute-start.3) | collective-permute-done | bytes 811040 | tf_op jit(solution)/shard_map/ppermute | solution.py:30
  43.1 7.8 %expert.3 = (bf16[192,2048]{1,0:T(8,128)(2,1)}, bf16[192,512]{1,0:T(8,128)(2,1)}, bf16[192,2048]{1,0:T(8,128)(2,1)}, bf16[192,1024]{1,0:T(8,128)(2,1)}, bf16[96,...) custom-call(bf16[96,4224]{1,0:T(8,128)(2,1)} %collective-permute-done.2.refs_0_, ...), custom_call_target="tpu_custom_call" | custom-call | flops 2415919104 | bytes 25165824 | tf_op jit(solution)/shard_map/expert/pallas_call | solution.py:79
  50.9 1.4 collective-permute-start.4
  52.9 7.8 %expert.2 = (bf16[192,2048]{1,0:T(8,128)(2,1)}, bf16[192,512]{1,0:T(8,128)(2,1)}, bf16[192,2048]{1,0:T(8,128)(2,1)}, bf16[192,1024]{1,0:T(8,128)(2,1)}, bf16[96,...) custom-call(bf16[96,4224]{1,0:T(8,128)(2,1)} %convolution_convert_fusion.3.refs_0_, ...), custom_call_target="tpu_custom_call" | custom-call | flops 2415919104 | bytes 25165824 | tf_op jit(solution)/shard_map/expert/pallas_call | solution.py:79
  61.0 2.8 %collective-permute-done.4 = bf16[96,2176]{1,0:T(8,128)(2,1)} collective-permute-done((bf16[96,2176]{1,0:T(8,128)(2,1)}, bf16[96,2176]{1,0:T(8,128)(2,1)}, u32[]{:S(2)}, u32[]{:S(2)}) %collective-permute-start.4) | collective-permute-done | bytes 417824 | tf_op jit(solution)/shard_map/ppermute | solution.py:30
  63.8 8.3 %collective-permute-done.5 = bf16[96,2176]{1,0:T(8,128)(2,1)} collective-permute-done((bf16[96,2176]{1,0:T(8,128)(2,1)}, bf16[96,2176]{1,0:T(8,128)(2,1)}, u32[]{:S(2)}, u32[]{:S(2)}) %collective-permute-start.5) | collective-permute-done | bytes 417824 | tf_op jit(solution)/shard_map/ppermute | solution.py:30
  72.1 1.7 fusion.8
  74.4 1.4 copy-done.2
  75.8 1.3 fusion
  77.0 2.0 %collective-permute-start.7 = (bf16[256,2048]{1,0:T(8,128)(2,1)}, bf16[256,2048]{1,0:T(8,128)(2,1)}, u32[]{:S(2)}, u32[]{:S(2)}) collective-permute-start(bf16[256,2048]{1,0:T(8,128)(2,1)} %fusion), channel_id=1, source_target_pairs={{0,2},{1,3},{2,0},{3,1},{4,6},{5,7},{6,4},{7,5},{8,10},{9,11},{10,... | collective-permute-start | bytes 3145736 | tf_op jit(solution)/shard_map/ppermute | solution.py:30
  79.1 0.9 copy.22
  80.0 0.8 copy.21
  80.8 4.4 %shard_map.170 = bf16[4,64,2048]{2,1,0:T(8,128)(2,1)} custom-call(s32[1]{0:T(128)} %bitcast.4.me_ref, bf16[512,192]{1,0:T(8,128)(2,1)} %bitcast.19, bf16[512,192]{1,0:T(8,128)(2,1)} %bitcast.15, bf16[192,2048]{1,0:T(8,128)(2,1)} %get-tuple-element.52.refs_2_, bf16[192,2048]{1,0:T(8,128)(2,1)} %get-tuple-element.53.refs_3_), custom_call_target="tpu_custom_call" | custom-call | flops 402653184 | bytes 2883584 | tf_op jit(solution)/shard_map/pallas_call | solution.py:157
  85.2 1.6 collective-permute-start.18
  86.8 4.2 %shard_map.162 = bf16[4,256,512]{2,1,0:T(8,128)(2,1)} custom-call(s32[1]{0:T(128)} %bitcast.4.me_ref, bf16[192,2048]{1,0:T(8,128)(2,1)} %get-tuple-element.40.refs_0_, bf16[192,2048]{1,0:T(8,128)(2,1)} %get-tuple-element.41.refs_1_, bf16[192,1024]{1,0:T(8,128)(2,1)} %get-tuple-element.42.refs_2_, bf16[192,1024]{1,0:T(8,128)(2,1)} %get-tuple-element.43.refs_3_), custom_call_target="tpu_custom_call" | custom-call | flops 402653184 | bytes 2293760 | tf_op jit(solution)/shard_map/pallas_call | solution.py:157
  90.9 1.5 collective-permute-start.12
  92.4 10.4 %collective-permute-done.7 = bf16[256,2048]{1,0:T(8,128)(2,1)} collective-permute-done((bf16[256,2048]{1,0:T(8,128)(2,1)}, bf16[256,2048]{1,0:T(8,128)(2,1)}, u32[]{:S(2)}, u32[]{:S(2)}) %collective-permute-start.7) | collective-permute-done | bytes 1048608 | tf_op jit(solution)/shard_map/ppermute | solution.py:30
  102.9 4.2 %shard_map.166 = bf16[4,256,512]{2,1,0:T(8,128)(2,1)} custom-call(s32[1]{0:T(128)} %bitcast.4.me_ref, bf16[192,2048]{1,0:T(8,128)(2,1)} %get-tuple-element.40.refs_0_, bf16[192,2048]{1,0:T(8,128)(2,1)} %get-tuple-element.41.refs_1_, bf16[192,1024]{1,0:T(8,128)(2,1)} %get-tuple-element.42.refs_2_, bf16[192,1024]{1,0:T(8,128)(2,1)} %get-tuple-element.43.refs_3_), custom_call_target="tpu_custom_call" | custom-call | flops 402653184 | bytes 2293760 | tf_op jit(solution)/shard_map/pallas_call | solution.py:157
  107.1 1.7 collective-permute-start.15
  108.7 1.0 broadcast_in_dim.8
  109.8 2.7 %fusion.1 = bf16[1024,512]{1,0:T(8,128)(2,1)} fusion(bf16[1024,512]{1,0:T(8,128)(2,1)} %broadcast_in_dim.8, s32[]{:T(128)S(6)} %select_n.12, bf16[256,2048]{1,0:T(8,128)(2,1)} %fusion, bf16[512,2048]{1,0:T(8,128)(2,1)S(1)} %copy-done), kind=kOutput, calls=%fused_computation.12 | convolution fusion | flops 537001984 | bytes 3407876 | tf_op jit(solution)/shard_map/dot_general | solution.py:20
  112.4 3.1 %shard_map.171 = bf16[2,64,2048]{2,1,0:T(8,128)(2,1)} custom-call(s32[1]{0:T(128)} %bitcast.4.me_ref, bf16[512,192]{1,0:T(8,128)(2,1)} %bitcast.20, bf16[512,192]{1,0:T(8,128)(2,1)} %bitcast.16, bf16[192,2048]{1,0:T(8,128)(2,1)} %get-tuple-element.52.refs_2_, bf16[192,2048]{1,0:T(8,128)(2,1)} %get-tuple-element.53.refs_3_, ...), custom_call_target="tpu_custom_call" | custom-call | flops 201326592 | bytes 1835008 | tf_op jit(solution)/shard_map/pallas_call | solution.py:157
  115.5 2.6 %collective-permute-start.19 = (bf16[2,64,2048]{2,1,0:T(8,128)(2,1)}, bf16[2,64,2048]{2,1,0:T(8,128)(2,1)}, u32[]{:S(2)}, u32[]{:S(2)}) collective-permute-start(bf16[2,64,2048]{2,1,0:T(8,128)(2,1)} %shard_map.171), channel_id=1, source_target_pairs={{0,16},{4,20},{8,24},{12,28},{16,0},{20,4},{24,8},{28,12},{1,17},{... | collective-permute-start | bytes 1572872 | tf_op jit(solution)/shard_map/ppermute | solution.py:30
  118.1 1.0 copy-done.1
  119.1 2.6 %shard_map.163 = bf16[2,256,512]{2,1,0:T(8,128)(2,1)} custom-call(s32[1]{0:T(128)} %bitcast.4.me_ref, bf16[192,2048]{1,0:T(8,128)(2,1)} %get-tuple-element.40.refs_0_, bf16[192,2048]{1,0:T(8,128)(2,1)} %get-tuple-element.41.refs_1_, bf16[192,1024]{1,0:T(8,128)(2,1)} %get-tuple-element.42.refs_2_, bf16[192,1024]{1,0:T(8,128)(2,1)} %get-tuple-element.43.refs_3_, ...), custom_call_target="tpu_custom_call" | custom-call | flops 201326592 | bytes 1245184 | tf_op jit(solution)/shard_map/pallas_call | solution.py:157
  121.7 1.6 collective-permute-start.13
  123.3 2.7 %fusion.2 = bf16[1024,512]{1,0:T(8,128)(2,1)} fusion(bf16[1024,512]{1,0:T(8,128)(2,1)} %fusion.1, s32[]{:T(128)S(6)} %select_n.13, bf16[256,2048]{1,0:T(8,128)(2,1)} %collective-permute-done.6, bf16[512,2048]{1,0:T(8,128)(2,1)S(1)} %copy-done), kind=kOutput, calls=%fused_computation.13 | convolution fusion | flops 537001984 | bytes 3407876 | tf_op jit(solution)/shard_map/dot_general | solution.py:20
  126.0 2.7 %fusion.3 = bf16[1024,512]{1,0:T(8,128)(2,1)} fusion(bf16[1024,512]{1,0:T(8,128)(2,1)} %fusion.2, s32[]{:T(128)S(6)} %select_n.14, bf16[256,2048]{1,0:T(8,128)(2,1)} %collective-permute-done.7, bf16[512,2048]{1,0:T(8,128)(2,1)S(1)} %copy-done), kind=kOutput, calls=%fused_computation.14 | convolution fusion | flops 537001984 | bytes 3407876 | tf_op jit(solution)/shard_map/dot_general | solution.py:20
  128.7 2.7 %fusion.4.grad_ref = bf16[1024,512]{1,0:T(8,128)(2,1)} fusion(bf16[1024,512]{1,0:T(8,128)(2,1)} %fusion.3, s32[]{:T(128)S(6)} %select_n.15, bf16[256,2048]{1,0:T(8,128)(2,1)} %collective-permute-done.8, bf16[512,2048]{1,0:T(8,128)(2,1)S(1)} %copy-done), kind=kOutput, calls=%fused_computation.15 | convolution fusion | flops 537001984 | bytes 3407876 | tf_op jit(solution)/shard_map/dot_general | solution.py:20
  131.3 1.0 broadcast_in_dim.11.inv_ref
  132.3 4.1 %state.1 = (f32[4,128,128]{2,1,0:T(8,128)}, bf16[1024,512]{1,0:T(8,128)(2,1)}) custom-call(bf16[1024,512]{1,0:T(8,128)(2,1)} %query_ref.3, bf16[1024,512]{1,0:T(8,128)(2,1)} %fusion.4.grad_ref, f32[1024,128]{1,0:T(8,128)} %broadcast_in_dim.11.inv_ref), custom_call_target="tpu_custom_call" | custom-call | flops 134217728 | bytes 3145728 | tf_op jit(solution)/shard_map/state/pallas_call | solution.py:317
  136.4 1.7 convert_element_type.75
  138.1 1.3 collective-permute-start.9
  139.4 2.7 %shard_map.167 = bf16[2,256,512]{2,1,0:T(8,128)(2,1)} custom-call(s32[1]{0:T(128)} %bitcast.4.me_ref, bf16[192,2048]{1,0:T(8,128)(2,1)} %get-tuple-element.40.refs_0_, bf16[192,2048]{1,0:T(8,128)(2,1)} %get-tuple-element.41.refs_1_, bf16[192,1024]{1,0:T(8,128)(2,1)} %get-tuple-element.42.refs_2_, bf16[192,1024]{1,0:T(8,128)(2,1)} %get-tuple-element.43.refs_3_, ...), custom_call_target="tpu_custom_call" | custom-call | flops 201326592 | bytes 1245184 | tf_op jit(solution)/shard_map/pallas_call | solution.py:157
  142.1 2.6 %collective-permute-start.16 = (bf16[2,256,512]{2,1,0:T(8,128)(2,1)}, bf16[2,256,512]{2,1,0:T(8,128)(2,1)S(1)}, u32[]{:S(2)}, u32[]{:S(2)}) collective-permute-start(bf16[2,256,512]{2,1,0:T(8,128)(2,1)} %shard_map.167), channel_id=1, source_target_pairs={{0,8},{4,12},{8,0},{12,4},{16,24},{20,28},{24,16},{28,20},{1,9},{5... | collective-permute-start | bytes 1572872 | tf_op jit(solution)/shard_map/ppermute | solution.py:30
  145.9 1.3 collective-permute-start.10
  147.2 2.7 %shard_map.172 = bf16[1,64,2048]{2,1,0:T(8,128)(2,1)} custom-call(s32[1]{0:T(128)} %bitcast.4.me_ref, bf16[512,192]{1,0:T(8,128)(2,1)} %bitcast.21, bf16[512,192]{1,0:T(8,128)(2,1)} %bitcast.17, bf16[192,2048]{1,0:T(8,128)(2,1)} %get-tuple-element.52.refs_2_, bf16[192,2048]{1,0:T(8,128)(2,1)} %get-tuple-element.53.refs_3_, ...), custom_call_target="tpu_custom_call" | custom-call | flops 100663296 | bytes 1310720 | tf_op jit(solution)/shard_map/pallas_call | solution.py:157
  149.9 5.9 %collective-permute-start.20 = (bf16[1,64,2048]{2,1,0:T(8,128)(2,1)}, bf16[1,64,2048]{2,1,0:T(8,128)(2,1)}, u32[]{:S(2)}, u32[]{:S(2)}) collective-permute-start(bf16[1,64,2048]{2,1,0:T(8,128)(2,1)} %shard_map.172), channel_id=1, source_target_pairs={{0,4},{4,0},{8,12},{12,8},{16,20},{20,16},{24,28},{28,24},{1,5},{5... | collective-permute-start | bytes 786440 | tf_op jit(solution)/shard_map/ppermute | solution.py:30
  155.8 0.8 copy-done.4
  156.6 2.4 %shard_map.164 = bf16[1,256,512]{2,1,0:T(8,128)(2,1)} custom-call(s32[1]{0:T(128)} %bitcast.4.me_ref, bf16[192,2048]{1,0:T(8,128)(2,1)} %get-tuple-element.40.refs_0_, bf16[192,2048]{1,0:T(8,128)(2,1)} %get-tuple-element.41.refs_1_, bf16[192,1024]{1,0:T(8,128)(2,1)} %get-tuple-element.42.refs_2_, bf16[192,1024]{1,0:T(8,128)(2,1)} %get-tuple-element.43.refs_3_, ...), custom_call_target="tpu_custom_call" | custom-call | flops 100663296 | bytes 720896 | tf_op jit(solution)/shard_map/pallas_call | solution.py:157
  159.2 5.4 %collective-permute-done.10 = bf16[4,128,128]{2,1,0:T(8,128)(2,1)} collective-permute-done((bf16[4,128,128]{2,1,0:T(8,128)(2,1)}, bf16[4,128,128]{2,1,0:T(8,128)(2,1)}, u32[]{:S(2)}, u32[]{:S(2)}) %collective-permute-start.10) | collective-permute-done | bytes 131104 | tf_op jit(solution)/shard_map/ppermute | solution.py:332
  164.6 1.6 add_convert_fusion
  166.2 1.3 collective-permute-start.11
  167.5 0.9 slice.15
  169.1 5.7 %forward.1 = bf16[1024,512]{1,0:T(8,128)(2,1)} custom-call(bf16[1024,512]{1,0:T(8,128)(2,1)} %key_ref.3, bf16[1024,512]{1,0:T(8,128)(2,1)} %value_ref.3, bf16[1024,512]{1,0:T(8,128)(2,1)} %fusion.4.grad_ref, f32[1024,128]{1,0:T(8,128)} %broadcast_in_dim.11.inv_ref, f32[4,128,128]{2,1,0:T(8,128)} %bitcast.23), custom_call_target="tpu_custom_call" | custom-call | flops 805306368 | bytes 4194304 | tf_op jit(solution)/shard_map/forward/pallas_call | solution.py:341
  174.7 1.1 collective-permute-done.14.refs_6_
  175.8 2.9 %shard_map.173 = f32[1,64,2048]{2,1,0:T(8,128)} custom-call(s32[1]{0:T(128)} %bitcast.4.me_ref, bf16[512,192]{1,0:T(8,128)(2,1)} %bitcast.22, bf16[512,192]{1,0:T(8,128)(2,1)} %bitcast.18, bf16[192,2048]{1,0:T(8,128)(2,1)} %get-tuple-element.52.refs_2_, bf16[192,2048]{1,0:T(8,128)(2,1)} %get-tuple-element.53.refs_3_, ...), custom_call_target="tpu_custom_call" | custom-call | flops 100663296 | bytes 1310720 | tf_op jit(solution)/shard_map/pallas_call | solution.py:157
  178.7 2.5 %shard_map.165 = f32[1,256,512]{2,1,0:T(8,128)} custom-call(s32[1]{0:T(128)} %bitcast.4.me_ref, bf16[192,2048]{1,0:T(8,128)(2,1)} %get-tuple-element.40.refs_0_, bf16[192,2048]{1,0:T(8,128)(2,1)} %get-tuple-element.41.refs_1_, bf16[192,1024]{1,0:T(8,128)(2,1)} %get-tuple-element.42.refs_2_, bf16[192,1024]{1,0:T(8,128)(2,1)} %get-tuple-element.43.refs_3_, ...), custom_call_target="tpu_custom_call" | custom-call | flops 100663296 | bytes 720896 | tf_op jit(solution)/shard_map/pallas_call | solution.py:157
  181.3 0.8 copy-done.5
  182.1 2.4 %shard_map.168 = bf16[1,256,512]{2,1,0:T(8,128)(2,1)} custom-call(s32[1]{0:T(128)} %bitcast.4.me_ref, bf16[192,2048]{1,0:T(8,128)(2,1)} %get-tuple-element.40.refs_0_, bf16[192,2048]{1,0:T(8,128)(2,1)} %get-tuple-element.41.refs_1_, bf16[192,1024]{1,0:T(8,128)(2,1)} %get-tuple-element.42.refs_2_, bf16[192,1024]{1,0:T(8,128)(2,1)} %get-tuple-element.43.refs_3_, ...), custom_call_target="tpu_custom_call" | custom-call | flops 100663296 | bytes 720896 | tf_op jit(solution)/shard_map/pallas_call | solution.py:157
  184.4 2.5 %collective-permute-start.17 = (bf16[1,256,512]{2,1,0:T(8,128)(2,1)}, bf16[1,256,512]{2,1,0:T(8,128)(2,1)S(1)}, u32[]{:S(2)}, u32[]{:S(2)}) collective-permute-start(bf16[1,256,512]{2,1,0:T(8,128)(2,1)} %shard_map.168), channel_id=1, source_target_pairs={{0,16},{4,20},{8,24},{12,28},{16,0},{20,4},{24,8},{28,12},{1,17},{... | collective-permute-start | bytes 786440 | tf_op jit(solution)/shard_map/ppermute | solution.py:30
  186.9 1.7 convert_add_fusion.2.later_ref
  188.6 7.2 %backward.1 = (bf16[1024,512]{1,0:T(8,128)(2,1)}, bf16[1024,512]{1,0:T(8,128)(2,1)}) custom-call(bf16[1024,512]{1,0:T(8,128)(2,1)} %query_ref.3, bf16[1024,512]{1,0:T(8,128)(2,1)} %key_ref.3, bf16[1024,512]{1,0:T(8,128)(2,1)} %value_ref.3, bf16[1024,512]{1,0:T(8,128)(2,1)} %get-tuple-element.36.scaled_ref, f32[4,128,128]{2,1,0:T(8,128)} %convert_add_fusion.2.later_ref), custom_call_target="tpu_custom_call" | custom-call | flops 1476395008 | bytes 6291456 | tf_op jit(solution)/shard_map/backward/pallas_call | solution.py:350
  195.7 1.2 collective-permute-done.17.refs_6_
  197.0 0.7 copy-done.10
  197.7 2.5 %shard_map.169 = f32[1,256,512]{2,1,0:T(8,128)} custom-call(s32[1]{0:T(128)} %bitcast.4.me_ref, bf16[192,2048]{1,0:T(8,128)(2,1)} %get-tuple-element.40.refs_0_, bf16[192,2048]{1,0:T(8,128)(2,1)} %get-tuple-element.41.refs_1_, bf16[192,1024]{1,0:T(8,128)(2,1)} %get-tuple-element.42.refs_2_, bf16[192,1024]{1,0:T(8,128)(2,1)} %get-tuple-element.43.refs_3_, ...), custom_call_target="tpu_custom_call" | custom-call | flops 100663296 | bytes 720896 | tf_op jit(solution)/shard_map/pallas_call | solution.py:157
  200.2 2.1 %pad_maximum_fusion.1 = f32[1,256,1024]{2,1,0:T(8,128)} fusion(f32[1,256,512]{2,1,0:T(8,128)} %shard_map.169, f32[1,256,512]{2,1,0:T(8,128)S(1)} %copy-done.6), kind=kLoop, calls=%fused_computation.16 | loop fusion | flops 262144 | bytes 2097152 | tf_op jit(solution)/shard_map/concatenate | solution.py:364
  (53 shorter events, 5.1 us)
Async XLA Ops:
  0.6 109.1 %copy-start = (bf16[512,2048]{1,0:T(8,128)(2,1)S(1)}, bf16[512,2048]{1,0:T(8,128)(2,1)}, u32[]{:S(2)}) copy-start(bf16[512,2048]{1,0:T(8,128)(2,1)} %param.21) | copy-start | bytes 6291460
  3.1 5.3 %copy-start.7 = (bf16[256,2048]{1,0:T(8,128)(2,1)S(1)}, bf16[256,2048]{1,0:T(8,128)(2,1)}, u32[]{:S(2)}) copy-start(bf16[256,2048]{1,0:T(8,128)(2,1)} %param.16) | copy-start | bytes 3145732
  3.1 5.3 %copy-start.13 = (bf16[256,2048]{1,0:T(8,128)(2,1)S(1)}, bf16[256,2048]{1,0:T(8,128)(2,1)}, u32[]{:S(2)}) copy-start(bf16[256,2048]{1,0:T(8,128)(2,1)} %param.15) | copy-start | bytes 3145732
  5.4 22.1 %collective-permute-start.2 = (bf16[96,4224]{1,0:T(8,128)(2,1)S(1)}, bf16[96,4224]{1,0:T(8,128)(2,1)}, u32[]{:S(2)}, u32[]{:S(2)}) collective-permute-start(bf16[96,4224]{1,0:T(8,128)(2,1)S(1)} %convolution_convert_fusion.1), channel_id=1, source_target_pairs={{0,2},{1,3},{2,0},{3,1},{4,6},{5,7},{6,4},{7,5},{8,10},{9,11},{10,... | collective-permute-start | bytes 2433032 | tf_op jit(solution)/shard_map/ppermute | solution.py:30
  9.0 34.2 %collective-permute-start.3 = (bf16[96,4224]{1,0:T(8,128)(2,1)S(1)}, bf16[96,4224]{1,0:T(8,128)(2,1)}, u32[]{:S(2)}, u32[]{:S(2)}) collective-permute-start(bf16[96,4224]{1,0:T(8,128)(2,1)S(1)} %convolution_convert_fusion), channel_id=1, source_target_pairs={{0,3},{1,2},{2,1},{3,0},{4,7},{5,6},{6,5},{7,4},{8,11},{9,10},{10,... | collective-permute-start | bytes 2433032 | tf_op jit(solution)/shard_map/ppermute | solution.py:30
  10.5 42.5 %collective-permute-start = (bf16[96,4224]{1,0:T(8,128)(2,1)}, bf16[96,4224]{1,0:T(8,128)(2,1)}, u32[]{:S(2)}, u32[]{:S(2)}) collective-permute-start(bf16[96,4224]{1,0:T(8,128)(2,1)} %convolution_convert_fusion.2), channel_id=1, source_target_pairs={{0,1},{1,0},{2,3},{3,2},{4,5},{5,4},{6,7},{7,6},{8,9},{9,8},{10,11... | collective-permute-start | bytes 2433032 | tf_op jit(solution)/shard_map/ppermute | solution.py:30
  50.9 12.8 %collective-permute-start.4 = (bf16[96,2176]{1,0:T(8,128)(2,1)}, bf16[96,2176]{1,0:T(8,128)(2,1)}, u32[]{:S(2)}, u32[]{:S(2)}) collective-permute-start(bf16[96,2176]{1,0:T(8,128)(2,1)} %get-tuple-element.34), channel_id=1, source_target_pairs={{0,2},{1,3},{2,0},{3,1},{4,6},{5,7},{6,4},{7,5},{8,10},{9,11},{10,... | collective-permute-start | bytes 1253384 | tf_op jit(solution)/shard_map/ppermute | solution.py:30
  52.4 19.7 %collective-permute-start.5 = (bf16[96,2176]{1,0:T(8,128)(2,1)}, bf16[96,2176]{1,0:T(8,128)(2,1)}, u32[]{:S(2)}, u32[]{:S(2)}) collective-permute-start(bf16[96,2176]{1,0:T(8,128)(2,1)} %get-tuple-element.35), channel_id=1, source_target_pairs={{0,3},{1,2},{2,1},{3,0},{4,7},{5,6},{6,5},{7,4},{8,11},{9,10},{10,... | collective-permute-start | bytes 1253384 | tf_op jit(solution)/shard_map/ppermute | solution.py:30
  60.7 13.1 %copy-start.8 = (bf16[96,2176]{1,0:T(8,128)(2,1)S(1)}, bf16[96,2176]{1,0:T(8,128)(2,1)}, u32[]{:S(2)}) copy-start(bf16[96,2176]{1,0:T(8,128)(2,1)} %get-tuple-element.32) | copy-start | bytes 1253380
  60.7 13.0 %collective-permute-start.1 = (bf16[96,2176]{1,0:T(8,128)(2,1)}, bf16[96,2176]{1,0:T(8,128)(2,1)S(1)}, u32[]{:S(2)}, u32[]{:S(2)}) collective-permute-start(bf16[96,2176]{1,0:T(8,128)(2,1)} %get-tuple-element.33), channel_id=1, source_target_pairs={{0,1},{1,0},{2,3},{3,2},{4,5},{5,4},{6,7},{7,6},{8,9},{9,8},{10,11... | collective-permute-start | bytes 1253384 | tf_op jit(solution)/shard_map/ppermute | solution.py:30
  74.4 1.4 copy-start.2
  75.8 3.3 %copy-start.11 = (bf16[192,512]{1,0:T(8,128)(2,1)S(1)}, bf16[192,512]{1,0:T(8,128)(2,1)}, u32[]{:S(2)}) copy-start(bf16[192,512]{1,0:T(8,128)(2,1)} %get-tuple-element.51) | copy-start | bytes 589828
  75.8 4.2 %copy-start.12 = (bf16[192,512]{1,0:T(8,128)(2,1)S(1)}, bf16[192,512]{1,0:T(8,128)(2,1)}, u32[]{:S(2)}) copy-start(bf16[192,512]{1,0:T(8,128)(2,1)} %get-tuple-element.50) | copy-start | bytes 589828
  77.0 25.8 %collective-permute-start.7 = (bf16[256,2048]{1,0:T(8,128)(2,1)}, bf16[256,2048]{1,0:T(8,128)(2,1)}, u32[]{:S(2)}, u32[]{:S(2)}) collective-permute-start(bf16[256,2048]{1,0:T(8,128)(2,1)} %fusion), channel_id=1, source_target_pairs={{0,2},{1,3},{2,0},{3,1},{4,6},{5,7},{6,4},{7,5},{8,10},{9,11},{10,... | collective-permute-start | bytes 3145736 | tf_op jit(solution)/shard_map/ppermute | solution.py:30
  85.2 27.2 %collective-permute-start.18 = (bf16[4,64,2048]{2,1,0:T(8,128)(2,1)}, bf16[4,64,2048]{2,1,0:T(8,128)(2,1)}, u32[]{:S(2)}, u32[]{:S(2)}) collective-permute-start(bf16[4,64,2048]{2,1,0:T(8,128)(2,1)} %shard_map.170), channel_id=1, source_target_pairs={{0,8},{4,12},{8,0},{12,4},{16,24},{20,28},{24,16},{28,20},{1,9},{5... | collective-permute-start | bytes 3145736 | tf_op jit(solution)/shard_map/ppermute | solution.py:30
  90.9 27.2 %collective-permute-start.12 = (bf16[4,256,512]{2,1,0:T(8,128)(2,1)}, bf16[4,256,512]{2,1,0:T(8,128)(2,1)S(1)}, u32[]{:S(2)}, u32[]{:S(2)}) collective-permute-start(bf16[4,256,512]{2,1,0:T(8,128)(2,1)} %shard_map.162), channel_id=1, source_target_pairs={{0,4},{4,0},{8,12},{12,8},{16,20},{20,16},{24,28},{28,24},{1,5},{5... | collective-permute-start | bytes 3145736 | tf_op jit(solution)/shard_map/ppermute | solution.py:30
  92.4 30.9 %collective-permute-start.6 = (bf16[256,2048]{1,0:T(8,128)(2,1)}, bf16[256,2048]{1,0:T(8,128)(2,1)}, u32[]{:S(2)}, u32[]{:S(2)}) collective-permute-start(bf16[256,2048]{1,0:T(8,128)(2,1)} %fusion), channel_id=1, source_target_pairs={{0,1},{1,0},{2,3},{3,2},{4,5},{5,4},{6,7},{7,6},{8,9},{9,8},{10,11... | collective-permute-start | bytes 3145736 | tf_op jit(solution)/shard_map/ppermute | solution.py:30
  102.8 25.8 %collective-permute-start.8 = (bf16[256,2048]{1,0:T(8,128)(2,1)}, bf16[256,2048]{1,0:T(8,128)(2,1)}, u32[]{:S(2)}, u32[]{:S(2)}) collective-permute-start(bf16[256,2048]{1,0:T(8,128)(2,1)} %collective-permute-done.7), channel_id=1, source_target_pairs={{0,1},{1,0},{2,3},{3,2},{4,5},{5,4},{6,7},{7,6},{8,9},{9,8},{10,11... | collective-permute-start | bytes 3145736 | tf_op jit(solution)/shard_map/ppermute | solution.py:30
  107.1 32.3 %collective-permute-start.15 = (bf16[4,256,512]{2,1,0:T(8,128)(2,1)}, bf16[4,256,512]{2,1,0:T(8,128)(2,1)}, u32[]{:S(2)}, u32[]{:S(2)}) collective-permute-start(bf16[4,256,512]{2,1,0:T(8,128)(2,1)} %shard_map.166), channel_id=1, source_target_pairs={{0,4},{4,0},{8,12},{12,8},{16,20},{20,16},{24,28},{28,24},{1,5},{5... | collective-permute-start | bytes 3145736 | tf_op jit(solution)/shard_map/ppermute | solution.py:30
  115.5 31.7 %collective-permute-start.19 = (bf16[2,64,2048]{2,1,0:T(8,128)(2,1)}, bf16[2,64,2048]{2,1,0:T(8,128)(2,1)}, u32[]{:S(2)}, u32[]{:S(2)}) collective-permute-start(bf16[2,64,2048]{2,1,0:T(8,128)(2,1)} %shard_map.171), channel_id=1, source_target_pairs={{0,16},{4,20},{8,24},{12,28},{16,0},{20,4},{24,8},{28,12},{1,17},{... | collective-permute-start | bytes 1572872 | tf_op jit(solution)/shard_map/ppermute | solution.py:30
  118.1 1.0 copy-start.1
  121.7 34.1 %collective-permute-start.13 = (bf16[2,256,512]{2,1,0:T(8,128)(2,1)}, bf16[2,256,512]{2,1,0:T(8,128)(2,1)S(1)}, u32[]{:S(2)}, u32[]{:S(2)}) collective-permute-start(bf16[2,256,512]{2,1,0:T(8,128)(2,1)} %shard_map.163), channel_id=1, source_target_pairs={{0,8},{4,12},{8,0},{12,4},{16,24},{20,28},{24,16},{28,20},{1,9},{5... | collective-permute-start | bytes 1572872 | tf_op jit(solution)/shard_map/ppermute | solution.py:30
  136.4 8.8 %copy-start.3 = (f32[4,128,128]{2,1,0:T(8,128)S(1)}, f32[4,128,128]{2,1,0:T(8,128)}, u32[]{:S(2)}) copy-start(f32[4,128,128]{2,1,0:T(8,128)} %get-tuple-element.37) | copy-start | bytes 786436
  138.1 7.1 %collective-permute-start.9 = (bf16[4,128,128]{2,1,0:T(8,128)(2,1)}, bf16[4,128,128]{2,1,0:T(8,128)(2,1)S(1)}, u32[]{:S(2)}, u32[]{:S(2)}) collective-permute-start(bf16[4,128,128]{2,1,0:T(8,128)(2,1)} %convert_element_type.75), channel_id=1, source_target_pairs={{4,0},{8,4},{12,8},{16,12},{20,16},{24,20},{28,24},{5,1},{9,5},{13... | collective-permute-start | bytes 393224 | tf_op jit(solution)/shard_map/ppermute | solution.py:332
  142.1 39.2 %collective-permute-start.16 = (bf16[2,256,512]{2,1,0:T(8,128)(2,1)}, bf16[2,256,512]{2,1,0:T(8,128)(2,1)S(1)}, u32[]{:S(2)}, u32[]{:S(2)}) collective-permute-start(bf16[2,256,512]{2,1,0:T(8,128)(2,1)} %shard_map.167), channel_id=1, source_target_pairs={{0,8},{4,12},{8,0},{12,4},{16,24},{20,28},{24,16},{28,20},{1,9},{5... | collective-permute-start | bytes 1572872 | tf_op jit(solution)/shard_map/ppermute | solution.py:30
  145.9 18.7 %collective-permute-start.10 = (bf16[4,128,128]{2,1,0:T(8,128)(2,1)}, bf16[4,128,128]{2,1,0:T(8,128)(2,1)}, u32[]{:S(2)}, u32[]{:S(2)}) collective-permute-start(bf16[4,128,128]{2,1,0:T(8,128)(2,1)} %fusion.12), channel_id=1, source_target_pairs={{8,0},{12,4},{16,8},{20,12},{24,16},{28,20},{9,1},{13,5},{17,9},{2... | collective-permute-start | bytes 393224 | tf_op jit(solution)/shard_map/ppermute | solution.py:332
  149.9 24.9 %collective-permute-start.20 = (bf16[1,64,2048]{2,1,0:T(8,128)(2,1)}, bf16[1,64,2048]{2,1,0:T(8,128)(2,1)}, u32[]{:S(2)}, u32[]{:S(2)}) collective-permute-start(bf16[1,64,2048]{2,1,0:T(8,128)(2,1)} %shard_map.172), channel_id=1, source_target_pairs={{0,4},{4,0},{8,12},{12,8},{16,20},{20,16},{24,28},{28,24},{1,5},{5... | collective-permute-start | bytes 786440 | tf_op jit(solution)/shard_map/ppermute | solution.py:30
  155.8 0.8 copy-start.4
  158.9 16.9 %collective-permute-start.14 = (bf16[1,256,512]{2,1,0:T(8,128)(2,1)}, bf16[1,256,512]{2,1,0:T(8,128)(2,1)S(1)}, u32[]{:S(2)}, u32[]{:S(2)}) collective-permute-start(bf16[1,256,512]{2,1,0:T(8,128)(2,1)} %shard_map.164), channel_id=1, source_target_pairs={{0,16},{4,20},{8,24},{12,28},{16,0},{20,4},{24,8},{28,12},{1,17},{... | collective-permute-start | bytes 786440 | tf_op jit(solution)/shard_map/ppermute | solution.py:30
  166.2 20.7 %collective-permute-start.11 = (bf16[4,128,128]{2,1,0:T(8,128)(2,1)}, bf16[4,128,128]{2,1,0:T(8,128)(2,1)S(1)}, u32[]{:S(2)}, u32[]{:S(2)}) collective-permute-start(bf16[4,128,128]{2,1,0:T(8,128)(2,1)} %add_convert_fusion), channel_id=1, source_target_pairs={{16,0},{20,4},{24,8},{28,12},{17,1},{21,5},{25,9},{29,13},{18,2},{... | collective-permute-start | bytes 393224 | tf_op jit(solution)/shard_map/ppermute | solution.py:332
  175.8 2.9 %copy-start.9 = (bf16[1,256,512]{2,1,0:T(8,128)(2,1)}, bf16[1,256,512]{2,1,0:T(8,128)(2,1)S(1)}, u32[]{:S(2)}) copy-start(bf16[1,256,512]{2,1,0:T(8,128)(2,1)S(1)} %collective-permute-done.14.refs_6_) | copy-start | bytes 786436
  181.3 0.8 copy-start.5
  184.4 12.5 %collective-permute-start.17 = (bf16[1,256,512]{2,1,0:T(8,128)(2,1)}, bf16[1,256,512]{2,1,0:T(8,128)(2,1)S(1)}, u32[]{:S(2)}, u32[]{:S(2)}) collective-permute-start(bf16[1,256,512]{2,1,0:T(8,128)(2,1)} %shard_map.168), channel_id=1, source_target_pairs={{0,16},{4,20},{8,24},{12,28},{16,0},{20,4},{24,8},{28,12},{1,17},{... | collective-permute-start | bytes 786440 | tf_op jit(solution)/shard_map/ppermute | solution.py:30
  195.7 4.4 %copy-start.6 = (f32[1,256,512]{2,1,0:T(8,128)S(1)}, f32[1,256,512]{2,1,0:T(8,128)}, u32[]{:S(2)}) copy-start(f32[1,256,512]{2,1,0:T(8,128)} %shard_map.165) | copy-start | bytes 1572868
  197.0 0.7 copy-start.10
where the time goes:
time: 204 us; the launch traced here: 202 us
  Pallas kernels  69 us (34%)
  waiting for transfers between devices  61 us (30%)
  starting transfers between devices  31.4 us (15%)
  matrix products  18.5 us (9%)
  other arithmetic  11.5 us (6%)
  local copies, waits for them, and re-layouts  10.1 us (5%)
    ppermute x18, waiting for transfers between devices, flip(): return lax.ppermute(value, axis, [(i, i ^ bit) for i in range(size)])  55 us
    pallas_call x12, Pallas kernels, step(): pl.pallas_call(functools.partial(partial_kernel, self.by_rows, parts), gr...  36.5 us
    ppermute x18, starting transfers between devices, flip(): return lax.ppermute(value, axis, [(i, i ^ bit) for i in range(size)])  27.6 us
    pallas_call x2, Pallas kernels, expert_backward(): pl.pallas_call(functools.partial(expert_kernel, near, width), in_specs=[w...  15.6 us
    dot_general x4, matrix products, contract_cols(): lax.dot_general(left, right, (((1,), (1,)), ((), ())), preferred_element_...  10.7 us
    pallas_call x1, Pallas kernels, compute(): pl.pallas_call(functools.partial(backward_kernel, chunk), grid=(heads,),...  7.17 us
    ppermute x3, waiting for transfers between devices, compute(): lax.ppermute(held, 'ctx', [(i, i - step) for i in range(step, blocks_tota...  5.94 us
    pallas_call x1, Pallas kernels, compute(): pl.pallas_call(functools.partial(forward_kernel, chunk), grid=(heads,), i...  5.67 us
  transfers between devices with their start and end apart: 21, of which 9 were waited for; matrix products, arithmetic and copies ran while one was open for 13% of the time, Pallas kernels for 33%

commit v1 on v0

--- a/solution.py
+++ b/solution.py
@@ -173,13 +173,39 @@
         return None
 
 
-def state_kernel(query_ref, grad_ref, inv_ref, state_ref, scaled_ref):
-    scaled = (grad_ref[...].astype(jnp.float32) * inv_ref[...]).astype(jnp.bfloat16)
-    scaled_ref[...] = scaled
-    state_ref[0] = contract_rows(query_ref[...], scaled)
-
-
-def forward_kernel(chunk, key_ref, value_ref, grad_ref, inv_ref, prior_ref, out_ref):
+def inverse_counts(place_ref, start, shape):
+    counts = place_ref[1] + start + 1 + lax.broadcasted_iota(jnp.int32, shape, 0)
+    return 1.0 / counts.astype(jnp.float32)
+
+
+def project_kernel(groups, place_ref, *refs):
+    pieces, (w_ref, query_ref), (grad_ref, scaled_ref, state_ref, sent_ref) = (
+        refs[:groups],
+        refs[groups : groups + 2],
+        refs[groups + 2 :],
+    )
+    rows = pieces[0].shape[0]
+    heads, head_dim = state_ref.shape[:2]
+    width = heads * head_dim
+    for k in range(groups):
+        start = pl.multiple_of((place_ref[0] ^ k) * rows, rows)
+        at = pl.ds(start, rows)
+        grads = contract_cols(pieces[k][...], w_ref[...]).astype(jnp.bfloat16)
+        inverse = inverse_counts(place_ref, start, (rows, width))
+        scaled = (grads.astype(jnp.float32) * inverse).astype(jnp.bfloat16)
+        grad_ref[at, :] = grads
+        scaled_ref[at, :] = scaled
+        for h in range(heads):
+            cols = slice(h * head_dim, (h + 1) * head_dim)
+            state = contract_rows(query_ref[at, cols], scaled[:, cols])
+            if k:
+                state = state + state_ref[h]
+            state_ref[h] = state
+            if k == groups - 1:
+                sent_ref[h] = state.astype(jnp.bfloat16)
+
+
+def forward_kernel(chunk, place_ref, key_ref, value_ref, grad_ref, prior_ref, out_ref):
     tokens = key_ref.shape[0]
     row = lax.broadcasted_iota(jnp.int32, (chunk, chunk), 0)
     col = lax.broadcasted_iota(jnp.int32, (chunk, chunk), 1)
@@ -189,7 +215,7 @@
         keys, values, grads = key_ref[rows, :], value_ref[rows, :], grad_ref[rows, :]
         mix = jnp.where(col <= row, contract_cols(grads, values), 0.0).astype(jnp.bfloat16)
         out = plain(mix, keys) + contract_cols(grads, state.astype(jnp.bfloat16))
-        out_ref[rows, :] = (out * inv_ref[rows, :]).astype(jnp.bfloat16)
+        out_ref[rows, :] = (out * inverse_counts(place_ref, at * chunk, out.shape)).astype(jnp.bfloat16)
         state = state + contract_rows(keys, values)
 
 
@@ -261,15 +287,14 @@
     by_rows = (width // blocks_total) % LANES != 0
     lefts = [part[0].T if by_rows else part[0] for part in parts]
     grad_boths = [part[3] for part in parts]
-    ups = [
-        ScatterSum(lefts, grad_boths, at, hidden_units, "ctx", rising, by_rows, width)
-        for at in range(2)
-    ]
+    up = ScatterSum(
+        lefts, grad_boths, 0, 2 * hidden_units, "ctx", rising, by_rows, width
+    )
     down = ScatterSum(
         [part[1].T for part in parts], [part[2] for part in parts],
         0, width, "ctx", turned, True, hidden_units,
     )
-    for one in (ups[0], down, ups[1]):
+    for one in (up, down):
         one.step()
 
     def unpack(low):
@@ -284,69 +309,57 @@
     grad_gates = pair_grads[:, width : width + 1].astype(jnp.bfloat16)
 
     pieces = {0: grad_resid}
-    heads_width = w_out.shape[0]
-    attn_grad = jnp.zeros((rows * groups, heads_width), jnp.bfloat16)
     for k in range(1, groups):
         low = k & -k
         pieces[k] = flip(pieces[k - low], "exp", low, groups)
-    for k in range(groups):
-        piece = contract_cols(pieces[k], w_out).astype(jnp.bfloat16)
-        attn_grad = lax.dynamic_update_slice(attn_grad, piece, ((mine ^ k) * rows, 0))
-        if k == 0:
-            ups[0].step(attn_grad)
-            down.step(attn_grad)
-    ups[1].step(attn_grad)
+    down.step(grad_resid)
 
     head_dim = prefix_state.shape[-1]
     tokens = attn_query.shape[0]
     heads = attn_query.shape[1] // head_dim
     block_at = lax.axis_index("ctx")
-    counts = (
-        3 * tokens * blocks_total + block_at * tokens + jnp.arange(tokens, dtype=jnp.int32) + 1
-    ).astype(jnp.float32)
-    inverse = jnp.broadcast_to((1.0 / counts)[:, None], (tokens, head_dim))
+    place = jnp.stack([mine, (3 * blocks_total + block_at) * tokens]).astype(jnp.int32)
 
     per_head = pl.BlockSpec((tokens, head_dim), lambda h: (0, h))
-    fixed = pl.BlockSpec((tokens, head_dim), lambda h: (0, 0))
+    scalars = pl.BlockSpec(memory_space=pltpu.SMEM)
+    whole = pl.BlockSpec(memory_space=pltpu.VMEM)
     one_state = pl.BlockSpec((1, head_dim, head_dim), lambda h: (h, 0, 0))
     flat = jax.ShapeDtypeStruct((tokens, heads * head_dim), jnp.bfloat16)
     states = jax.ShapeDtypeStruct((heads, head_dim, head_dim), jnp.float32)
     chunk = min(256, tokens)
 
     size = 2 * tokens * heads * head_dim
-    local_state, grad_scaled = pl.pallas_call(
-        state_kernel,
-        grid=(heads,),
-        in_specs=[per_head, per_head, fixed],
-        out_specs=[one_state, per_head],
-        out_shape=[states, flat],
-        cost_estimate=cost(size * head_dim, 3 * size),
-        name="state",
-    )(attn_query, attn_grad, inverse)
+    attn_grad, grad_scaled, local_state, held = pl.pallas_call(
+        functools.partial(project_kernel, groups),
+        in_specs=[scalars] + [whole] * (groups + 2),
+        out_specs=[whole] * 4,
+        out_shape=[flat, flat, states, jax.ShapeDtypeStruct(states.shape, jnp.bfloat16)],
+        cost_estimate=cost(size * (width + head_dim), 4 * size + 2 * tokens * width),
+        name="project",
+    )(place, *[pieces[k] for k in range(groups)], w_out, attn_query)
 
     later = jnp.zeros_like(local_state)
     step = 1
     results = {}
     while step < blocks_total:
+        came = lax.ppermute(held, "ctx", [(i, i - step) for i in range(step, blocks_total)])
+        if step == 1:
+            up.step(held)
+        elif step == 2:
+            results["down"] = down.step(held)
+        later = later + came.astype(jnp.float32)
         held = (local_state + later).astype(jnp.bfloat16)
-        came = lax.ppermute(held, "ctx", [(i, i - step) for i in range(step, blocks_total)])
-        for name, one in (("up0", ups[0]), ("down", down), ("up1", ups[1])):
-            if name not in results and (name != "up1" or step > 1):
-                got = one.step(held)
-                if got is not None:
-                    results[name] = got
-        later = later + came.astype(jnp.float32)
         step *= 2
 
     grad_query = pl.pallas_call(
         functools.partial(forward_kernel, chunk),
         grid=(heads,),
-        in_specs=[per_head, per_head, per_head, fixed, one_state],
+        in_specs=[scalars, per_head, per_head, per_head, one_state],
         out_specs=per_head,
         out_shape=flat,
         cost_estimate=cost(size * (2 * chunk + 2 * head_dim), 4 * size),
         name="forward",
-    )(attn_key, attn_value, attn_grad, inverse, prefix_state[0])
+    )(place, attn_key, attn_value, attn_grad, prefix_state[0])
     grad_key, grad_value = pl.pallas_call(
         functools.partial(backward_kernel, chunk),
         grid=(heads,),
@@ -356,13 +369,10 @@
         cost_estimate=cost(size * (4 * chunk + 3 * head_dim), 6 * size),
         name="backward",
     )(attn_query, attn_key, attn_value, grad_scaled, later)
-    for name, one in (("up0", ups[0]), ("down", down), ("up1", ups[1])):
-        while name not in results:
-            got = one.step()
-            if got is not None:
-                results[name] = got
-    grad_gate_up = jnp.concatenate([results["up0"], results["up1"]], axis=2)
-    grad_down = results["down"]
+    for name, one in (("up", up), ("down", down)):
+        while results.get(name) is None:
+            results[name] = one.step()
+    grad_gate_up, grad_down = results["up"], results["down"]
     return grad_query, grad_key, grad_value, grad_resid, grad_gates, grad_gate_up, grad_down
 
 

time: 204 us -> 226 us (1.11)
  waiting for transfers between devices: 61 us -> 111 us
  matrix products: 18.5 us -> 5.77 us
  other arithmetic: 11.5 us -> 5.03 us
  Pallas kernels: 69 us -> 62.8 us
  starting transfers between devices: 31.4 us -> 28.6 us
    ppermute x18 -> x15, waiting for transfers between devices: 55 us -> 90.4 us  [flip(): return lax.ppermute(value, axis, [(i, i ^ bit) for i in range(size)])]
    ppermute x3, waiting for transfers between devices: 5.94 us -> 20.3 us  [compute(): lax.ppermute(held, 'ctx', [(i, i - step) for i in range(step, blocks_tota...]
    dot_general x4 -> x0, matrix products: 10.7 us -> none  [contract_cols(): lax.dot_general(left, right, (((1,), (1,)), ((), ())), preferred_element_...]
    pallas_call x12 -> x8, Pallas kernels: 36.5 us -> 27.1 us  [step(): pl.pallas_call(functools.partial(partial_kernel, self.by_rows, parts), gr...]
    convert_element_type x3 -> x2, other arithmetic: 3.98 us -> 0.08 us  [compute(): held = (local_state + later).astype(jnp.bfloat16)]
    pallas_call x1, Pallas kernels: 4.07 us -> 7.71 us  [compute(): pl.pallas_call(functools.partial(project_kernel, groups), in_specs=[scala...]
    unnamed x29 -> x33, local copies, waits for them, and re-layouts: 5.34 us -> 8.58 us
    ppermute x18 -> x15, starting transfers between devices: 27.6 us -> 24.7 us  [flip(): return lax.ppermute(value, axis, [(i, i ^ bit) for i in range(size)])]
  transfers between devices with their start and end apart: 21 -> 18, of which waited for: 9 -> 9; matrix products, arithmetic and copies ran while one was open for 13% -> 3% of each run, Pallas kernels for 33% -> 27%
where the time goes in v1:
time: 226 us; the launch traced here: 225 us
  waiting for transfers between devices  111 us (49%)
  Pallas kernels  62.8 us (28%)
  starting transfers between devices  28.6 us (13%)
  local copies, waits for them, and re-layouts  11.3 us (5%)
  matrix products  5.77 us (3%)
  other arithmetic  5.03 us (2%)
    ppermute x15, waiting for transfers between devices, flip(): return lax.ppermute(value, axis, [(i, i ^ bit) for i in range(size)])  90.4 us
    pallas_call x8, Pallas kernels, step(): pl.pallas_call(functools.partial(partial_kernel, self.by_rows, parts), gr...  27.1 us
    ppermute x15, starting transfers between devices, flip(): return lax.ppermute(value, axis, [(i, i ^ bit) for i in range(size)])  24.7 us
    ppermute x3, waiting for transfers between devices, compute(): lax.ppermute(held, 'ctx', [(i, i - step) for i in range(step, blocks_tota...  20.3 us
    pallas_call x2, Pallas kernels, expert_backward(): pl.pallas_call(functools.partial(expert_kernel, near, width), in_specs=[w...  15.6 us
    unnamed x33, local copies, waits for them, and re-layouts  8.58 us
    pallas_call x1, Pallas kernels, compute(): pl.pallas_call(functools.partial(project_kernel, groups), in_specs=[scala...  7.71 us
    pallas_call x1, Pallas kernels, compute(): pl.pallas_call(functools.partial(backward_kernel, chunk), grid=(heads,),...  7.17 us
  transfers between devices with their start and end apart: 18, of which 9 were waited for; matrix products, arithmetic and copies ran while one was open for 3% of the time, Pallas kernels for 27%

profile of v1, /device:TPU:0, one launch (start us, length us, event | category | flops | bytes accessed | tf_op | source)
XLA Modules:
  0.0 225.0 jit_solution(4414505699110625441)
XLA Ops:
  0.6 0.9 convert_reduce_fusion
  1.5 0.7 reduce
  2.2 0.7 multiply_add_fusion
  2.9 0.1 broadcast_in_dim.5
  3.0 2.2 convolution_convert_fusion.1
  5.3 3.1 %collective-permute-start.2 = (bf16[96,4224]{1,0:T(8,128)(2,1)S(1)}, bf16[96,4224]{1,0:T(8,128)(2,1)S(1)}, u32[]{:S(2)}, u32[]{:S(2)}) collective-permute-start(bf16[96,4224]{1,0:T(8,128)(2,1)S(1)} %convolution_convert_fusion.1), channel_id=1, source_target_pairs={{0,2},{1,3},{2,0},{3,1},{4,6},{5,7},{6,4},{7,5},{8,10},{9,11},{10,... | collective-permute-start | bytes 2433032 | tf_op jit(solution)/shard_map/ppermute | solution.py:30
  8.3 0.5 convolution_convert_fusion
  8.9 0.1 collective-permute-start.3
  8.9 0.5 convolution_convert_fusion.2
  9.5 0.2 collective-permute-start
  9.7 1.4 convolution_convert_fusion.3.refs_0_
  11.1 16.2 %collective-permute-done.2.refs_0_ = bf16[96,4224]{1,0:T(8,128)(2,1)S(1)} collective-permute-done((bf16[96,4224]{1,0:T(8,128)(2,1)S(1)}, bf16[96,4224]{1,0:T(8,128)(2,1)S(1)}, u32[]{:S(2)}, u32[]{:S(2)}) %collective-permute-start.2) | collective-permute-done | bytes 811040 | tf_op jit(solution)/shard_map/ppermute | solution.py:30
  27.2 15.8 %collective-permute-done.3.refs_1_ = bf16[96,4224]{1,0:T(8,128)(2,1)} collective-permute-done((bf16[96,4224]{1,0:T(8,128)(2,1)S(1)}, bf16[96,4224]{1,0:T(8,128)(2,1)}, u32[]{:S(2)}, u32[]{:S(2)}) %collective-permute-start.3) | collective-permute-done | bytes 811040 | tf_op jit(solution)/shard_map/ppermute | solution.py:30
  43.0 7.8 %expert.3 = (bf16[192,2048]{1,0:T(8,128)(2,1)}, bf16[192,512]{1,0:T(8,128)(2,1)}, bf16[192,2048]{1,0:T(8,128)(2,1)}, bf16[192,1024]{1,0:T(8,128)(2,1)}, bf16[96,...) custom-call(bf16[96,4224]{1,0:T(8,128)(2,1)} %copy-done.14, bf16[96,4224]{1,0:T(8,128)(2,1)} %collective-permute-done.3.refs_1_, ...), custom_call_target="tpu_custom_call" | custom-call | flops 2415919104 | bytes 25165824 | tf_op jit(solution)/shard_map/expert/pallas_call | solution.py:79
  50.8 1.5 collective-permute-start.4
  52.3 0.6 collective-permute-start.5
  52.8 0.9 copy-done.13
  53.7 7.8 %expert.2 = (bf16[192,2048]{1,0:T(8,128)(2,1)}, bf16[192,512]{1,0:T(8,128)(2,1)}, bf16[192,2048]{1,0:T(8,128)(2,1)}, bf16[192,1024]{1,0:T(8,128)(2,1)}, bf16[96,...) custom-call(bf16[96,4224]{1,0:T(8,128)(2,1)} %convolution_convert_fusion.3.refs_0_, bf16[96,4224]{1,0:T(8,128)(2,1)} %copy-done.13, ...), custom_call_target="tpu_custom_call" | custom-call | flops 2415919104 | bytes 25165824 | tf_op jit(solution)/shard_map/expert/pallas_call | solution.py:79
  61.5 0.1 collective-permute-start.1
  61.6 0.1 iota_compare_fusion.1
  61.7 1.8 collective-permute-done.4
  63.5 8.3 %collective-permute-done.5 = bf16[96,2176]{1,0:T(8,128)(2,1)S(1)} collective-permute-done((bf16[96,2176]{1,0:T(8,128)(2,1)}, bf16[96,2176]{1,0:T(8,128)(2,1)S(1)}, u32[]{:S(2)}, u32[]{:S(2)}) %collective-permute-start.5) | collective-permute-done | bytes 417824 | tf_op jit(solution)/shard_map/ppermute | solution.py:30
  71.9 0.6 fusion.4
  72.5 0.6 convolution_add_fusion
  73.0 1.4 copy-done.2
  74.4 1.3 fusion.refs_0_
  75.7 2.0 collective-permute-start.7
  77.7 4.9 %shard_map.162 = bf16[4,256,1024]{2,1,0:T(8,128)(2,1)} custom-call(s32[1]{0:T(128)} %bitcast.6.me_ref, bf16[192,2048]{1,0:T(8,128)(2,1)} %get-tuple-element.38.refs_0_, bf16[192,2048]{1,0:T(8,128)(2,1)} %get-tuple-element.39.refs_1_, bf16[192,1024]{1,0:T(8,128)(2,1)} %get-tuple-element.40.refs_2_, bf16[192,1024]{1,0:T(8,128)(2,1)} %get-tuple-element.41.refs_3_), custom_call_target="tpu_custom_call" | custom-call | flops 805306368 | bytes 4587520 | tf_op jit(solution)/shard_map/pallas_call | solution.py:157
  82.7 1.5 collective-permute-start.12
  84.1 17.4 %collective-permute-done.7.refs_2_ = bf16[256,2048]{1,0:T(8,128)(2,1)} collective-permute-done((bf16[256,2048]{1,0:T(8,128)(2,1)}, bf16[256,2048]{1,0:T(8,128)(2,1)}, u32[]{:S(2)}, u32[]{:S(2)}) %collective-permute-start.7) | collective-permute-done | bytes 1048608 | tf_op jit(solution)/shard_map/ppermute | solution.py:30
  101.5 0.8 copy.22
  102.3 0.9 copy.21
  103.2 4.4 %shard_map.166 = bf16[4,64,2048]{2,1,0:T(8,128)(2,1)} custom-call(s32[1]{0:T(128)} %bitcast.6.me_ref, bf16[512,192]{1,0:T(8,128)(2,1)} %bitcast.13, bf16[512,192]{1,0:T(8,128)(2,1)} %bitcast.9, bf16[192,2048]{1,0:T(8,128)(2,1)} %get-tuple-element.45.refs_2_, bf16[192,2048]{1,0:T(8,128)(2,1)} %get-tuple-element.46.refs_3_), custom_call_target="tpu_custom_call" | custom-call | flops 402653184 | bytes 2883584 | tf_op jit(solution)/shard_map/pallas_call | solution.py:157
  107.6 1.7 collective-permute-start.15
  109.3 0.6 pad_add_fusion.place_ref
  109.9 7.7 %project.1 = (bf16[1024,512]{1,0:T(8,128)(2,1)}, bf16[1024,512]{1,0:T(8,128)(2,1)}, f32[4,128,128]{2,1,0:T(8,128)}, bf16[4,128,128]{2,1,0:T(8,128)(2,1)}) custom-call(s32[2]{0:T(128)} %pad_add_fusion.place_ref, bf16[256,2048]{1,0:T(8,128)(2,1)} %fusion.refs_0_, bf16[256,2048]{1,0:T(8,128)(2,1)} %collective-permute-done.6.refs_1_, ...), custom_call_target="tpu_custom_call" | custom-call | flops 2281701376 | bytes 8388608 | tf_op jit(solution)/shard_map/project/pallas_call | solution.py:332
  117.6 12.6 %collective-permute-done.12.refs_4_ = bf16[4,256,1024]{2,1,0:T(8,128)(2,1)S(1)} collective-permute-done((bf16[4,256,1024]{2,1,0:T(8,128)(2,1)}, bf16[4,256,1024]{2,1,0:T(8,128)(2,1)S(1)}, u32[]{:S(2)}, u32[]{:S(2)}) %collective-permute-start.12) | collective-permute-done | bytes 2097184 | tf_op jit(solution)/shard_map/ppermute | solution.py:30
  130.2 1.3 copy-done
  131.6 3.2 %shard_map.163 = bf16[2,256,1024]{2,1,0:T(8,128)(2,1)} custom-call(s32[1]{0:T(128)} %bitcast.6.me_ref, bf16[192,2048]{1,0:T(8,128)(2,1)} %get-tuple-element.38.refs_0_, bf16[192,2048]{1,0:T(8,128)(2,1)} %get-tuple-element.39.refs_1_, bf16[192,1024]{1,0:T(8,128)(2,1)} %get-tuple-element.40.refs_2_, bf16[192,1024]{1,0:T(8,128)(2,1)} %get-tuple-element.41.refs_3_, ...), custom_call_target="tpu_custom_call" | custom-call | flops 402653184 | bytes 2490368 | tf_op jit(solution)/shard_map/pallas_call | solution.py:157
  134.8 1.6 collective-permute-start.13
  136.4 1.0 copy-done.1
  137.4 3.1 %shard_map.167 = bf16[2,64,2048]{2,1,0:T(8,128)(2,1)} custom-call(s32[1]{0:T(128)} %bitcast.6.me_ref, bf16[512,192]{1,0:T(8,128)(2,1)} %bitcast.14, bf16[512,192]{1,0:T(8,128)(2,1)} %bitcast.10, bf16[192,2048]{1,0:T(8,128)(2,1)} %get-tuple-element.45.refs_2_, bf16[192,2048]{1,0:T(8,128)(2,1)} %get-tuple-element.46.refs_3_, bf16[4,64,2048]{2,1,0:T(8,128)(2,1)} %copy-done.1), custom_call_target="tpu_custom_call" | custom-call | flops 201326592 | bytes 1835008 | tf_op jit(solution)/shard_map/pallas_call | solution.py:157
  140.5 2.6 %collective-permute-start.16 = (bf16[2,64,2048]{2,1,0:T(8,128)(2,1)}, bf16[2,64,2048]{2,1,0:T(8,128)(2,1)S(1)}, u32[]{:S(2)}, u32[]{:S(2)}) collective-permute-start(bf16[2,64,2048]{2,1,0:T(8,128)(2,1)} %shard_map.167), channel_id=1, source_target_pairs={{0,16},{4,20},{8,24},{12,28},{16,0},{20,4},{24,8},{28,12},{1,17},{... | collective-permute-start | bytes 1572872 | tf_op jit(solution)/shard_map/ppermute | solution.py:30
  143.0 1.3 collective-permute-start.9
  144.3 5.6 %collective-permute-done.9 = bf16[4,128,128]{2,1,0:T(8,128)(2,1)S(1)} collective-permute-done((bf16[4,128,128]{2,1,0:T(8,128)(2,1)S(1)}, bf16[4,128,128]{2,1,0:T(8,128)(2,1)S(1)}, u32[]{:S(2)}, u32[]{:S(2)}) %collective-permute-start.9) | collective-permute-done | bytes 131104 | tf_op jit(solution)/shard_map/ppermute | solution.py:345
  149.9 1.3 collective-permute-start.10
  151.2 18.3 %collective-permute-done.16.refs_5_ = bf16[2,64,2048]{2,1,0:T(8,128)(2,1)S(1)} collective-permute-done((bf16[2,64,2048]{2,1,0:T(8,128)(2,1)}, bf16[2,64,2048]{2,1,0:T(8,128)(2,1)S(1)}, u32[]{:S(2)}, u32[]{:S(2)}) %collective-permute-start.16) | collective-permute-done | bytes 524320 | tf_op jit(solution)/shard_map/ppermute | solution.py:30
  169.5 0.8 copy-done.4
  170.3 2.6 %shard_map.168 = bf16[1,64,2048]{2,1,0:T(8,128)(2,1)} custom-call(s32[1]{0:T(128)} %bitcast.6.me_ref, bf16[512,192]{1,0:T(8,128)(2,1)} %bitcast.15, bf16[512,192]{1,0:T(8,128)(2,1)} %bitcast.11, bf16[192,2048]{1,0:T(8,128)(2,1)} %get-tuple-element.45.refs_2_, bf16[192,2048]{1,0:T(8,128)(2,1)} %get-tuple-element.46.refs_3_, bf16[4,64,2048]{2,1,0:T(8,128)(2,1)} %copy-done.1, ...), custom_call_target="tpu_custom_call" | custom-call | flops 100663296 | bytes 1310720 | tf_op jit(solution)/shard_map/pallas_call | solution.py:157
  173.0 6.4 %collective-permute-start.17 = (bf16[1,64,2048]{2,1,0:T(8,128)(2,1)}, bf16[1,64,2048]{2,1,0:T(8,128)(2,1)S(1)}, u32[]{:S(2)}, u32[]{:S(2)}) collective-permute-start(bf16[1,64,2048]{2,1,0:T(8,128)(2,1)} %shard_map.168), channel_id=1, source_target_pairs={{0,4},{4,0},{8,12},{12,8},{16,20},{20,16},{24,28},{28,24},{1,5},{5... | collective-permute-start | bytes 786440 | tf_op jit(solution)/shard_map/ppermute | solution.py:30
  179.4 1.0 copy-done.3
  180.4 2.8 %shard_map.164 = bf16[1,256,1024]{2,1,0:T(8,128)(2,1)} custom-call(s32[1]{0:T(128)} %bitcast.6.me_ref, bf16[192,2048]{1,0:T(8,128)(2,1)} %get-tuple-element.38.refs_0_, bf16[192,2048]{1,0:T(8,128)(2,1)} %get-tuple-element.39.refs_1_, bf16[192,1024]{1,0:T(8,128)(2,1)} %get-tuple-element.40.refs_2_, bf16[192,1024]{1,0:T(8,128)(2,1)} %get-tuple-element.41.refs_3_, ...), custom_call_target="tpu_custom_call" | custom-call | flops 201326592 | bytes 1441792 | tf_op jit(solution)/shard_map/pallas_call | solution.py:157
  183.2 3.4 %collective-permute-start.14 = (bf16[1,256,1024]{2,1,0:T(8,128)(2,1)}, bf16[1,256,1024]{2,1,0:T(8,128)(2,1)S(1)}, u32[]{:S(2)}, u32[]{:S(2)}) collective-permute-start(bf16[1,256,1024]{2,1,0:T(8,128)(2,1)} %shard_map.164), channel_id=1, source_target_pairs={{0,16},{4,20},{8,24},{12,28},{16,0},{20,4},{24,8},{28,12},{1,17},{... | collective-permute-start | bytes 1572872 | tf_op jit(solution)/shard_map/ppermute | solution.py:30
  186.7 1.3 collective-permute-start.11
  188.0 0.9 slice.15
  188.9 0.7 copy.23
  189.5 5.3 %forward.1 = bf16[1024,512]{1,0:T(8,128)(2,1)} custom-call(s32[2]{0:T(128)} %pad_add_fusion.place_ref, bf16[1024,512]{1,0:T(8,128)(2,1)} %key_ref.3, bf16[1024,512]{1,0:T(8,128)(2,1)} %value_ref.3, bf16[1024,512]{1,0:T(8,128)(2,1)} %get-tuple-element.32.grad_ref, f32[4,128,128]{2,1,0:T(8,128)} %bitcast.17), custom_call_target="tpu_custom_call" | custom-call | flops 805306368 | bytes 4194304 | tf_op jit(solution)/shard_map/forward/pallas_call | solution.py:354
  194.8 0.7 copy-done.9
  195.5 2.8 %shard_map.169 = f32[1,64,2048]{2,1,0:T(8,128)} custom-call(s32[1]{0:T(128)} %bitcast.6.me_ref, bf16[512,192]{1,0:T(8,128)(2,1)} %bitcast.16, bf16[512,192]{1,0:T(8,128)(2,1)} %bitcast.12, bf16[192,2048]{1,0:T(8,128)(2,1)} %get-tuple-element.45.refs_2_, bf16[192,2048]{1,0:T(8,128)(2,1)} %get-tuple-element.46.refs_3_, bf16[4,64,2048]{2,1,0:T(8,128)(2,1)} %copy-done.1, ...), custom_call_target="tpu_custom_call" | custom-call | flops 100663296 | bytes 1310720 | tf_op jit(solution)/shard_map/pallas_call | solution.py:157
  198.4 14.8 %collective-permute-done.11 = bf16[4,128,128]{2,1,0:T(8,128)(2,1)S(1)} collective-permute-done((bf16[4,128,128]{2,1,0:T(8,128)(2,1)S(1)}, bf16[4,128,128]{2,1,0:T(8,128)(2,1)S(1)}, u32[]{:S(2)}, u32[]{:S(2)}) %collective-permute-start.11) | collective-permute-done | bytes 131104 | tf_op jit(solution)/shard_map/ppermute | solution.py:345
  213.1 0.7 convert_add_fusion.2.later_ref
  213.9 7.2 %backward.1 = (bf16[1024,512]{1,0:T(8,128)(2,1)}, bf16[1024,512]{1,0:T(8,128)(2,1)}) custom-call(bf16[1024,512]{1,0:T(8,128)(2,1)} %query_ref.1, bf16[1024,512]{1,0:T(8,128)(2,1)} %key_ref.3, bf16[1024,512]{1,0:T(8,128)(2,1)} %value_ref.3, bf16[1024,512]{1,0:T(8,128)(2,1)} %get-tuple-element.33.scaled_ref, f32[4,128,128]{2,1,0:T(8,128)} %convert_add_fusion.2.later_ref), custom_call_target="tpu_custom_call" | custom-call | flops 1476395008 | bytes 6291456 | tf_op jit(solution)/shard_map/backward/pallas_call | solution.py:363
  221.1 0.8 copy-done.7
  221.9 3.2 %shard_map.165 = f32[1,256,1024]{2,1,0:T(8,128)} custom-call(s32[1]{0:T(128)} %bitcast.6.me_ref, bf16[192,2048]{1,0:T(8,128)(2,1)} %get-tuple-element.38.refs_0_, bf16[192,2048]{1,0:T(8,128)(2,1)} %get-tuple-element.39.refs_1_, bf16[192,1024]{1,0:T(8,128)(2,1)} %get-tuple-element.40.refs_2_, bf16[192,1024]{1,0:T(8,128)(2,1)} %get-tuple-element.41.refs_3_, ...), custom_call_target="tpu_custom_call" | custom-call | flops 201326592 | bytes 1441792 | tf_op jit(solution)/shard_map/pallas_call | solution.py:157
  (39 shorter events, 0.2 us)
Async XLA Ops:
  3.0 5.3 %copy-start.6 = (bf16[256,2048]{1,0:T(8,128)(2,1)S(1)}, bf16[256,2048]{1,0:T(8,128)(2,1)}, u32[]{:S(2)}) copy-start(bf16[256,2048]{1,0:T(8,128)(2,1)} %param.16) | copy-start | bytes 3145732
  3.0 5.3 %copy-start.12 = (bf16[256,2048]{1,0:T(8,128)(2,1)S(1)}, bf16[256,2048]{1,0:T(8,128)(2,1)}, u32[]{:S(2)}) copy-start(bf16[256,2048]{1,0:T(8,128)(2,1)} %param.15) | copy-start | bytes 3145732
  5.3 22.0 %collective-permute-start.2 = (bf16[96,4224]{1,0:T(8,128)(2,1)S(1)}, bf16[96,4224]{1,0:T(8,128)(2,1)S(1)}, u32[]{:S(2)}, u32[]{:S(2)}) collective-permute-start(bf16[96,4224]{1,0:T(8,128)(2,1)S(1)} %convolution_convert_fusion.1), channel_id=1, source_target_pairs={{0,2},{1,3},{2,0},{3,1},{4,6},{5,7},{6,4},{7,5},{8,10},{9,11},{10,... | collective-permute-start | bytes 2433032 | tf_op jit(solution)/shard_map/ppermute | solution.py:30
  8.9 34.2 %collective-permute-start.3 = (bf16[96,4224]{1,0:T(8,128)(2,1)S(1)}, bf16[96,4224]{1,0:T(8,128)(2,1)}, u32[]{:S(2)}, u32[]{:S(2)}) collective-permute-start(bf16[96,4224]{1,0:T(8,128)(2,1)S(1)} %convolution_convert_fusion), channel_id=1, source_target_pairs={{0,3},{1,2},{2,1},{3,0},{4,7},{5,6},{6,5},{7,4},{8,11},{9,10},{10,... | collective-permute-start | bytes 2433032 | tf_op jit(solution)/shard_map/ppermute | solution.py:30
  9.5 43.3 %collective-permute-start = (bf16[96,4224]{1,0:T(8,128)(2,1)S(1)}, bf16[96,4224]{1,0:T(8,128)(2,1)S(1)}, u32[]{:S(2)}, u32[]{:S(2)}) collective-permute-start(bf16[96,4224]{1,0:T(8,128)(2,1)S(1)} %convolution_convert_fusion.2), channel_id=1, source_target_pairs={{0,1},{1,0},{2,3},{3,2},{4,5},{5,4},{6,7},{7,6},{8,9},{9,8},{10,11... | collective-permute-start | bytes 2433032 | tf_op jit(solution)/shard_map/ppermute | solution.py:30
  27.2 15.8 %copy-start.14 = (bf16[96,4224]{1,0:T(8,128)(2,1)}, bf16[96,4224]{1,0:T(8,128)(2,1)S(1)}, u32[]{:S(2)}) copy-start(bf16[96,4224]{1,0:T(8,128)(2,1)S(1)} %collective-permute-done.2.refs_0_) | copy-start | bytes 2433028
  50.8 12.7 %collective-permute-start.4 = (bf16[96,2176]{1,0:T(8,128)(2,1)}, bf16[96,2176]{1,0:T(8,128)(2,1)S(1)}, u32[]{:S(2)}, u32[]{:S(2)}) collective-permute-start(bf16[96,2176]{1,0:T(8,128)(2,1)} %get-tuple-element.30), channel_id=1, source_target_pairs={{0,2},{1,3},{2,0},{3,1},{4,6},{5,7},{6,4},{7,5},{8,10},{9,11},{10,... | collective-permute-start | bytes 1253384 | tf_op jit(solution)/shard_map/ppermute | solution.py:30
  52.3 19.6 %collective-permute-start.5 = (bf16[96,2176]{1,0:T(8,128)(2,1)}, bf16[96,2176]{1,0:T(8,128)(2,1)S(1)}, u32[]{:S(2)}, u32[]{:S(2)}) collective-permute-start(bf16[96,2176]{1,0:T(8,128)(2,1)} %get-tuple-element.31), channel_id=1, source_target_pairs={{0,3},{1,2},{2,1},{3,0},{4,7},{5,6},{6,5},{7,4},{8,11},{9,10},{10,... | collective-permute-start | bytes 1253384 | tf_op jit(solution)/shard_map/ppermute | solution.py:30
  52.8 0.9 copy-start.13
  61.5 11.0 %copy-start.8 = (bf16[96,2176]{1,0:T(8,128)(2,1)S(1)}, bf16[96,2176]{1,0:T(8,128)(2,1)}, u32[]{:S(2)}) copy-start(bf16[96,2176]{1,0:T(8,128)(2,1)} %get-tuple-element.28) | copy-start | bytes 1253380
  61.5 11.0 %collective-permute-start.1 = (bf16[96,2176]{1,0:T(8,128)(2,1)}, bf16[96,2176]{1,0:T(8,128)(2,1)S(1)}, u32[]{:S(2)}, u32[]{:S(2)}) collective-permute-start(bf16[96,2176]{1,0:T(8,128)(2,1)} %get-tuple-element.29), channel_id=1, source_target_pairs={{0,1},{1,0},{2,3},{3,2},{4,5},{5,4},{6,7},{7,6},{8,9},{9,8},{10,11... | collective-permute-start | bytes 1253384 | tf_op jit(solution)/shard_map/ppermute | solution.py:30
  73.0 1.4 copy-start.2
  75.7 25.8 %collective-permute-start.7 = (bf16[256,2048]{1,0:T(8,128)(2,1)}, bf16[256,2048]{1,0:T(8,128)(2,1)}, u32[]{:S(2)}, u32[]{:S(2)}) collective-permute-start(bf16[256,2048]{1,0:T(8,128)(2,1)} %fusion.refs_0_), channel_id=1, source_target_pairs={{0,2},{1,3},{2,0},{3,1},{4,6},{5,7},{6,4},{7,5},{8,10},{9,11},{10,... | collective-permute-start | bytes 3145736 | tf_op jit(solution)/shard_map/ppermute | solution.py:30
  77.7 23.8 %copy-start.10 = (bf16[192,512]{1,0:T(8,128)(2,1)S(1)}, bf16[192,512]{1,0:T(8,128)(2,1)}, u32[]{:S(2)}) copy-start(bf16[192,512]{1,0:T(8,128)(2,1)} %get-tuple-element.44) | copy-start | bytes 589828
  77.7 24.6 %copy-start.11 = (bf16[192,512]{1,0:T(8,128)(2,1)S(1)}, bf16[192,512]{1,0:T(8,128)(2,1)}, u32[]{:S(2)}) copy-start(bf16[192,512]{1,0:T(8,128)(2,1)} %get-tuple-element.43) | copy-start | bytes 589828
  82.7 47.6 %collective-permute-start.12 = (bf16[4,256,1024]{2,1,0:T(8,128)(2,1)}, bf16[4,256,1024]{2,1,0:T(8,128)(2,1)S(1)}, u32[]{:S(2)}, u32[]{:S(2)}) collective-permute-start(bf16[4,256,1024]{2,1,0:T(8,128)(2,1)} %shard_map.162), channel_id=1, source_target_pairs={{0,4},{4,0},{8,12},{12,8},{16,20},{20,16},{24,28},{28,24},{1,5},{5... | collective-permute-start | bytes 6291464 | tf_op jit(solution)/shard_map/ppermute | solution.py:30
  84.1 25.8 %collective-permute-start.6 = (bf16[256,2048]{1,0:T(8,128)(2,1)}, bf16[256,2048]{1,0:T(8,128)(2,1)}, u32[]{:S(2)}, u32[]{:S(2)}) collective-permute-start(bf16[256,2048]{1,0:T(8,128)(2,1)} %fusion.refs_0_), channel_id=1, source_target_pairs={{0,1},{1,0},{2,3},{3,2},{4,5},{5,4},{6,7},{7,6},{8,9},{9,8},{10,11... | collective-permute-start | bytes 3145736 | tf_op jit(solution)/shard_map/ppermute | solution.py:30
  101.5 8.4 %collective-permute-start.8 = (bf16[256,2048]{1,0:T(8,128)(2,1)}, bf16[256,2048]{1,0:T(8,128)(2,1)}, u32[]{:S(2)}, u32[]{:S(2)}) collective-permute-start(bf16[256,2048]{1,0:T(8,128)(2,1)} %collective-permute-done.7.refs_2_), channel_id=1, source_target_pairs={{0,1},{1,0},{2,3},{3,2},{4,5},{5,4},{6,7},{7,6},{8,9},{9,8},{10,11... | collective-permute-start | bytes 3145736 | tf_op jit(solution)/shard_map/ppermute | solution.py:30
  107.6 28.8 %collective-permute-start.15 = (bf16[4,64,2048]{2,1,0:T(8,128)(2,1)}, bf16[4,64,2048]{2,1,0:T(8,128)(2,1)S(1)}, u32[]{:S(2)}, u32[]{:S(2)}) collective-permute-start(bf16[4,64,2048]{2,1,0:T(8,128)(2,1)} %shard_map.166), channel_id=1, source_target_pairs={{0,8},{4,12},{8,0},{12,4},{16,24},{20,28},{24,16},{28,20},{1,9},{5... | collective-permute-start | bytes 3145736 | tf_op jit(solution)/shard_map/ppermute | solution.py:30
  130.2 1.3 copy-start
  134.8 8.3 %copy-start.15 = (bf16[4,128,128]{2,1,0:T(8,128)(2,1)S(1)}, bf16[4,128,128]{2,1,0:T(8,128)(2,1)}, u32[]{:S(2)}) copy-start(bf16[4,128,128]{2,1,0:T(8,128)(2,1)} %get-tuple-element.34) | copy-start | bytes 393220
  134.8 15.1 %copy-start.5 = (f32[4,128,128]{2,1,0:T(8,128)S(1)}, f32[4,128,128]{2,1,0:T(8,128)}, u32[]{:S(2)}) copy-start(f32[4,128,128]{2,1,0:T(8,128)} %get-tuple-element.35) | copy-start | bytes 786436
  134.8 44.6 %collective-permute-start.13 = (bf16[2,256,1024]{2,1,0:T(8,128)(2,1)}, bf16[2,256,1024]{2,1,0:T(8,128)(2,1)S(1)}, u32[]{:S(2)}, u32[]{:S(2)}) collective-permute-start(bf16[2,256,1024]{2,1,0:T(8,128)(2,1)} %shard_map.163), channel_id=1, source_target_pairs={{0,8},{4,12},{8,0},{12,4},{16,24},{20,28},{24,16},{28,20},{1,9},{5... | collective-permute-start | bytes 3145736 | tf_op jit(solution)/shard_map/ppermute | solution.py:30
  136.4 1.0 copy-start.1
  140.5 29.0 %collective-permute-start.16 = (bf16[2,64,2048]{2,1,0:T(8,128)(2,1)}, bf16[2,64,2048]{2,1,0:T(8,128)(2,1)S(1)}, u32[]{:S(2)}, u32[]{:S(2)}) collective-permute-start(bf16[2,64,2048]{2,1,0:T(8,128)(2,1)} %shard_map.167), channel_id=1, source_target_pairs={{0,16},{4,20},{8,24},{12,28},{16,0},{20,4},{24,8},{28,12},{1,17},{... | collective-permute-start | bytes 1572872 | tf_op jit(solution)/shard_map/ppermute | solution.py:30
  143.0 6.8 %collective-permute-start.9 = (bf16[4,128,128]{2,1,0:T(8,128)(2,1)S(1)}, bf16[4,128,128]{2,1,0:T(8,128)(2,1)S(1)}, u32[]{:S(2)}, u32[]{:S(2)}) collective-permute-start(bf16[4,128,128]{2,1,0:T(8,128)(2,1)S(1)} %copy-done.15), channel_id=1, source_target_pairs={{4,0},{8,4},{12,8},{16,12},{20,16},{24,20},{28,24},{5,1},{9,5},{13... | collective-permute-start | bytes 393224 | tf_op jit(solution)/shard_map/ppermute | solution.py:345
  149.9 36.7 %collective-permute-start.10 = (bf16[4,128,128]{2,1,0:T(8,128)(2,1)S(1)}, bf16[4,128,128]{2,1,0:T(8,128)(2,1)S(1)}, u32[]{:S(2)}, u32[]{:S(2)}) collective-permute-start(bf16[4,128,128]{2,1,0:T(8,128)(2,1)S(1)} %fusion.8), channel_id=1, source_target_pairs={{8,0},{12,4},{16,8},{20,12},{24,16},{28,20},{9,1},{13,5},{17,9},{2... | collective-permute-start | bytes 393224 | tf_op jit(solution)/shard_map/ppermute | solution.py:345
  169.5 0.8 copy-start.4
  173.0 21.9 %collective-permute-start.17 = (bf16[1,64,2048]{2,1,0:T(8,128)(2,1)}, bf16[1,64,2048]{2,1,0:T(8,128)(2,1)S(1)}, u32[]{:S(2)}, u32[]{:S(2)}) collective-permute-start(bf16[1,64,2048]{2,1,0:T(8,128)(2,1)} %shard_map.168), channel_id=1, source_target_pairs={{0,4},{4,0},{8,12},{12,8},{16,20},{20,16},{24,28},{28,24},{1,5},{5... | collective-permute-start | bytes 786440 | tf_op jit(solution)/shard_map/ppermute | solution.py:30
  179.4 1.0 copy-start.3
  183.2 37.8 %collective-permute-start.14 = (bf16[1,256,1024]{2,1,0:T(8,128)(2,1)}, bf16[1,256,1024]{2,1,0:T(8,128)(2,1)S(1)}, u32[]{:S(2)}, u32[]{:S(2)}) collective-permute-start(bf16[1,256,1024]{2,1,0:T(8,128)(2,1)} %shard_map.164), channel_id=1, source_target_pairs={{0,16},{4,20},{8,24},{12,28},{16,0},{20,4},{24,8},{28,12},{1,17},{... | collective-permute-start | bytes 1572872 | tf_op jit(solution)/shard_map/ppermute | solution.py:30
  186.7 26.5 %collective-permute-start.11 = (bf16[4,128,128]{2,1,0:T(8,128)(2,1)S(1)}, bf16[4,128,128]{2,1,0:T(8,128)(2,1)S(1)}, u32[]{:S(2)}, u32[]{:S(2)}) collective-permute-start(bf16[4,128,128]{2,1,0:T(8,128)(2,1)S(1)} %add_convert_fusion), channel_id=1, source_target_pairs={{16,0},{20,4},{24,8},{28,12},{17,1},{21,5},{25,9},{29,13},{18,2},{... | collective-permute-start | bytes 393224 | tf_op jit(solution)/shard_map/ppermute | solution.py:345
  194.8 0.7 copy-start.9
  221.1 0.8 copy-start.7
